TPU v7x, 256 devices: a whole 4x4x8 slice. The times are simulated.
256 devices in a mesh: expert: 16 (over z, core), latent: 8 (over y, x_lo), row: 2 (over x_hi).
Axes of the slice: x: 4 (x_hi: 2, x_lo: 2; x = x_hi * 2 + x_lo), y: 4, z: 8, core: 2. Of those that a mesh axis runs over, the one named last changes fastest.
Arguments:
- model_acts: bfloat16 [512, 8192], P('row', 'expert'), may hold values from -6 to 6
- enc_weight: bfloat16 [8192, 12288], P('expert', ('latent', 'row')), may hold values from -0.0625 to 0.0625
- dec_weight: bfloat16 [12288, 8192], P(('latent', 'row'), 'expert'), may hold values from -0.0546875 to 0.0546875
- enc_bias: float32 [12288], P('latent'), may hold values from -3 to 3
- dec_bias: float32 [8192], P('expert'), may hold values from -3 to 3
- enc_first: bfloat16 [8192, 12288], P('expert', ('latent', 'row')), may hold values from -0.119628906 to 0.119628906
- enc_second: bfloat16 [8192, 12288], P('expert', ('latent', 'row')), may hold values from 9.9658966e-05 to 0.0099487305
- dec_first: bfloat16 [12288, 8192], P(('latent', 'row'), 'expert'), may hold values from -0.119628906 to 0.119628906
- dec_second: bfloat16 [12288, 8192], P(('latent', 'row'), 'expert'), may hold values from 9.9658966e-05 to 0.0099487305
Outputs:
- encoder_next: bfloat16 [8192, 12288], P('expert', ('latent', 'row'))
- decoder_next: bfloat16 [12288, 8192], P(('latent', 'row'), 'expert')
- enc_first_next: bfloat16 [8192, 12288], P('expert', ('latent', 'row'))
- enc_second_next: bfloat16 [8192, 12288], P('expert', ('latent', 'row'))
- dec_first_next: bfloat16 [12288, 8192], P(('latent', 'row'), 'expert')
- dec_second_next: bfloat16 [12288, 8192], P(('latent', 'row'), 'expert')
- enc_bias_grad: float32 [12288], P(('latent', 'row'))
- dec_bias_grad: float32 [8192], P('expert')
All inputs are finite; a program needn't handle non-finite values.
Results may differ from a plain program's by a relative error of at most 0.005.
Values may be sent and summed in bfloat16 or wider, within the bound.
A program may use at most 64 MiB of HBM per device.

v0:
```python
import jax
import jax.numpy as jnp
from jax import lax
from jax.sharding import PartitionSpec as P

EXPERTS = 8
D = 1024


beta_one = 0.9
beta_two = 0.999
learn_rate = 0.001
adam_eps = 1e-08
bias_one = 0.9999734386011124
bias_two = 0.09520785288629115
norm_eps = 1e-06
sparsity = 1.0


def sent_to_all(array, axis):
    peers = lax.axis_size(axis)
    return lax.all_to_all(
        jnp.broadcast_to(array[None], (peers, *array.shape)), axis, 0, 0, tiled=True
    )


def in_order(parts, dim):
    parts = jnp.moveaxis(parts, 0, dim)
    shape = parts.shape
    return parts.reshape(*shape[:dim], shape[dim] * shape[dim + 1], *shape[dim + 2 :])


def collect(array, axis, dim):
    parts = sent_to_all(array, axis)
    return in_order(parts, dim)


def total_of_pieces(array, axis):
    parts = lax.all_gather(array, axis)
    return parts.sum(axis=0)


def in_blocks(array, dim, peers):
    shape = array.shape
    parts = array.reshape(*shape[:dim], peers, shape[dim] // peers, *shape[dim + 1 :])
    return jnp.moveaxis(parts, dim, 0)


def sent_and_summed(array, axis, dim):
    peers = lax.axis_size(axis)
    parts = lax.all_to_all(in_blocks(array, dim, peers), axis, 0, 0, tiled=True)
    return jnp.sum(parts, axis=0)


def padded_to(lines, peers):
    spare = -lines.shape[0] % peers
    if not spare:
        return lines
    return jnp.concatenate([lines, jnp.zeros((spare, *lines.shape[1:]), lines.dtype)])


def nested_sum(array, axes):
    lines = array.reshape(-1, array.shape[-1])
    own = sent_and_summed(padded_to(lines, lax.axis_size(axes)), axes, 0)
    whole = collect(own, axes, 0)
    return whole[: len(lines)].reshape(array.shape)


def adam_step(weight, moment_one, moment_two, gradient):
    first_next = beta_one * moment_one.astype(jnp.float32) + (1.0 - beta_one) * gradient
    second_next = beta_two * moment_two.astype(jnp.float32) + (1.0 - beta_two) * gradient * gradient
    stepped = weight.astype(jnp.float32) - learn_rate * (first_next / bias_one) / (
        jnp.sqrt(second_next / bias_two) + adam_eps
    )
    return (
        stepped.astype(jnp.bfloat16),
        first_next.astype(jnp.bfloat16),
        second_next.astype(jnp.bfloat16),
    )


def contract_rows(left, right):
    return lax.dot_general(
        left, right, (((0,), (0,)), ((), ())), preferred_element_type=jnp.float32
    )


def local(
    model_acts,
    enc_weight,
    dec_weight,
    enc_bias,
    dec_bias,
    enc_first,
    enc_second,
    dec_first,
    dec_second,
):
    shard_width = model_acts.shape[1]
    local_latents = enc_weight.shape[1]
    total_rows = model_acts.shape[0] * lax.axis_size("row")
    row_index = lax.axis_index("row")
    token_rows = collect(model_acts, "row", 0)
    bias_here = lax.dynamic_slice_in_dim(enc_bias, row_index * local_latents, local_latents)
    column_pick = (jnp.arange(EXPERTS) == lax.axis_index("expert") * shard_width // D).astype(
        jnp.float32
    )
    decoder_wide = dec_weight.astype(jnp.float32)
    partial_sq = jnp.sum(decoder_wide * decoder_wide, axis=1)
    norm_sq = total_of_pieces(partial_sq[:, None] * column_pick[None, :], "expert")
    decoder_norms = jnp.sqrt(norm_sq + norm_eps)
    strength = jnp.sum(decoder_norms, axis=1)
    own_norm = jnp.sum(decoder_norms * column_pick[None, :], axis=1)
    preact_part = jnp.dot(token_rows, enc_weight, preferred_element_type=jnp.float32)
    preact = sent_and_summed(preact_part, "expert", 0) + bias_here
    active = preact > 0
    latent_low = collect(jnp.maximum(preact, 0.0).astype(jnp.bfloat16), "expert", 0)
    rebuilt_part = jnp.dot(latent_low, dec_weight, preferred_element_type=jnp.float32)
    rebuilt = nested_sum(rebuilt_part, ("latent", "row"))
    grad_rows = 2.0 * (rebuilt + dec_bias - token_rows.astype(jnp.float32)) / total_rows
    grad_low = grad_rows.astype(jnp.bfloat16)
    dec_main = contract_rows(latent_low, grad_low)
    col_total = jnp.sum(latent_low.astype(jnp.float32), axis=0)
    row_bias = jnp.sum(grad_rows, axis=0)
    back_part = lax.dot_general(
        grad_low, dec_weight, (((1,), (1,)), ((), ())), preferred_element_type=jnp.float32
    )
    penalty = sparsity * strength / total_rows
    back_grad = sent_and_summed(back_part, "expert", 0) + penalty
    grad_pre = collect(jnp.where(active, back_grad, 0.0).astype(jnp.bfloat16), "expert", 0)
    enc_main = contract_rows(token_rows, grad_pre)
    bias_sum = jnp.sum(grad_pre.astype(jnp.float32), axis=0)
    dec_grad = dec_main + sparsity * (col_total / total_rows)[:, None] * (
        dec_weight.astype(jnp.float32) / own_norm[:, None]
    )
    encoder_next, enc_first_next, enc_second_next = adam_step(
        enc_weight, enc_first, enc_second, enc_main
    )
    decoder_next, dec_first_next, dec_second_next = adam_step(
        dec_weight, dec_first, dec_second, dec_grad
    )
    return (
        encoder_next,
        decoder_next,
        enc_first_next,
        enc_second_next,
        dec_first_next,
        dec_second_next,
        bias_sum,
        row_bias,
    )


def solution(mesh):
    return jax.shard_map(
        local,
        mesh=mesh,
        in_specs=(
            P("row", "expert"),
            P("expert", ("latent", "row")),
            P(("latent", "row"), "expert"),
            P("latent"),
            P("expert"),
            P("expert", ("latent", "row")),
            P("expert", ("latent", "row")),
            P(("latent", "row"), "expert"),
            P(("latent", "row"), "expert"),
        ),
        out_specs=(
            P("expert", ("latent", "row")),
            P(("latent", "row"), "expert"),
            P("expert", ("latent", "row")),
            P("expert", ("latent", "row")),
            P(("latent", "row"), "expert"),
            P(("latent", "row"), "expert"),
            P(("latent", "row")),
            P("expert"),
        ),
        check_vma=False,
    )
```

profile of v0, /device:TPU:1, one launch (start us, length us, event | category | flops | bytes accessed | tf_op | source)
XLA Modules:
  0.0 232.4 jit_solution(8892236956337695387)
XLA Ops:
  0.6 1.1 broadcast_in_dim.9
  1.7 13.1 %all_to_all.35 = bf16[2,256,512]{2,1,0:T(8,128)(2,1)S(1)} all-to-all(bf16[2,256,512]{2,1,0:T(8,128)(2,1)S(1)} %broadcast_in_dim.9), channel_id=1, replica_groups=mesh['expert'=16,'latent'=8,'row'=2] {'row'}, dimensions={0} | all-to-all | bytes 1048576 | tf_op jit(solution)/shard_map/all_to_all | solution.py:22
  14.8 1.7 fusion.15
  16.6 10.5 %all-to-all-start.1 = ((f32[16,32,768]{2,1,0:T(8,128)}), f32[16,32,768]{2,1,0:T(8,128)S(1)}, u32[]{:S(2)}, u32[]{:S(2)}) async-start(f32[16,32,768]{2,1,0:T(8,128)} %fusion.15), calls=%async_computation.1 | async-start | bytes 3145728 | tf_op jit(solution)/shard_map/all_to_all | solution.py:51
  27.2 38.3 %all-to-all-done.1 = f32[16,32,768]{2,1,0:T(8,128)S(1)} async-done(((f32[16,32,768]{2,1,0:T(8,128)}), f32[16,32,768]{2,1,0:T(8,128)S(1)}, u32[]{:S(2)}, u32[]{:S(2)}) %all-to-all-start.1) | async-done | bytes 1572896 | tf_op jit(solution)/shard_map/all_to_all | solution.py:51
  65.8 27.1 %all_to_all.36 = bf16[16,32,768]{2,1,0:T(8,128)(2,1)S(1)} all-to-all(bf16[16,32,768]{2,1,0:T(8,128)(2,1)S(1)} %broadcast_in_dim.10), channel_id=1, replica_groups=mesh['expert'=16,'latent'=8,'row'=2] {'expert'}, dimensions={0} | all-to-all | bytes 1572864 | tf_op jit(solution)/shard_map/all_to_all | solution.py:22
  92.9 0.6 fusion.13
  93.5 20.1 %all_to_all.37 = f32[16,32,512]{2,1,0:T(8,128)S(1)} all-to-all(f32[16,32,512]{2,1,0:T(8,128)S(1)} %fusion.13), channel_id=1, replica_groups=mesh['expert'=16,'latent'=8,'row'=2] {'latent','row'}, dimensions={0} | all-to-all | bytes 2097152 | tf_op jit(solution)/shard_map/all_to_all | solution.py:51
  113.6 0.1 broadcast_in_dim.11
  113.7 18.5 %all_to_all.38 = f32[16,32,512]{2,1,0:T(8,128)S(1)} all-to-all(f32[16,32,512]{2,1,0:T(8,128)S(1)} %broadcast_in_dim.11), channel_id=1, replica_groups=mesh['expert'=16,'latent'=8,'row'=2] {'latent','row'}, dimensions={0} | all-to-all | bytes 2097152 | tf_op jit(solution)/shard_map/all_to_all | solution.py:22
  132.2 0.8 fusion.17
  133.0 0.8 copy-done.5
  133.8 1.8 fusion.11
  135.6 6.5 %all-to-all-start.5 = ((f32[16,32,768]{2,1,0:T(8,128)}), f32[16,32,768]{2,1,0:T(8,128)S(1)}, u32[]{:S(2)}, u32[]{:S(2)}) async-start(f32[16,32,768]{2,1,0:T(8,128)} %fusion.11), calls=%async_computation.5 | async-start | bytes 3145728 | tf_op jit(solution)/shard_map/all_to_all | solution.py:51
  142.1 0.2 fusion
  142.4 49.2 %all_gather.4 = f32[16,768,8]{1,2,0:T(8,128)S(1)} all-gather(f32[1,768,8]{1,2,0:T(8,128)S(1)} %broadcast_multiply_fusion), channel_id=1, replica_groups=mesh['expert'=16,'latent'=8,'row'=2] {'expert'}, dimensions={0}, use_global_device_ids=true | all-gather | bytes 417792 | tf_op jit(solution)/shard_map/all_gather | solution.py:39
  191.6 0.6 reduce_sum.94
  192.3 0.8 multiply_reduce_fusion
  193.2 0.1 reduce_sum.92
  193.3 1.0 broadcast_in_dim.12
  194.3 6.0 %all-to-all-start.6 = ((bf16[16,32,768]{2,1,0:T(8,128)(2,1)}), bf16[16,32,768]{2,1,0:T(8,128)(2,1)S(1)}, u32[]{:S(2)}, u32[]{:S(2)}) async-start(bf16[16,32,768]{2,1,0:T(8,128)(2,1)} %broadcast_in_dim.12), calls=%async_computation.6 | async-start | bytes 1572864 | tf_op jit(solution)/shard_map/all_to_all | solution.py:22
  200.2 1.2 copy.35
  201.4 2.3 copy.36
  203.7 2.3 %copy.37 = bf16[512,768]{0,1:T(8,128)(2,1)} copy(bf16[512,768]{1,0:T(8,128)(2,1)} %param.15) | data formatting | bytes 1572864 | tf_op args[6]
  206.0 0.1 convert_reduce_fusion.1
  206.2 4.7 %fusion.9 = (bf16[768,512]{1,0:T(8,128)(2,1)}, bf16[768,512]{1,0:T(8,128)(2,1)}, bf16[768,512]{1,0:T(8,128)(2,1)}) fusion(bf16[768,512]{1,0:T(8,128)(2,1)} %param.17, bf16[768,512]{1,0:T(8,128)(2,1)} %param.16, bf16[768,512]{1,0:T(8,128)(2,1)S(1)} %copy-done, f32[768]{0:T(1024)S(1)} %get-tuple-element.40, f32[768]{0:T(1024)S(1)} %broadcast_multiply_fusion.1, ...), kind=kOutput, calls=%fused_computation.20 | convolution fusion | flops 410910720 | bytes 6035456 | tf_op jit(solution)/shard_map/dot_general | solution.py:83
  210.9 12.0 %all-to-all-done.6 = bf16[16,32,768]{2,1,0:T(8,128)(2,1)S(1)} async-done(((bf16[16,32,768]{2,1,0:T(8,128)(2,1)}), bf16[16,32,768]{2,1,0:T(8,128)(2,1)S(1)}, u32[]{:S(2)}, u32[]{:S(2)}) %all-to-all-start.6) | async-done | bytes 786464 | tf_op jit(solution)/shard_map/all_to_all | solution.py:22
  222.9 4.1 %fusion.10 = (bf16[512,768]{0,1:T(8,128)(2,1)S(1)}, bf16[512,768]{0,1:T(8,128)(2,1)}, bf16[512,768]{0,1:T(8,128)(2,1)S(1)}) fusion(bf16[512,768]{0,1:T(8,128)(2,1)} %copy.37, bf16[512,768]{0,1:T(8,128)(2,1)} %copy.36, bf16[512,768]{0,1:T(8,128)(2,1)} %copy.35, bf16[512,768]{1,0:T(8,128)(2,1)S(1)} %bitcast.36, bf16[512,512]{1,0:T(8,128)(2,1)S(1)} %bitcast.35), kind=kOutput, calls=%fused_computation.21 | convolution fusion | flops 409731072 | bytes 6029312 | tf_op jit(solution)/shard_map/dot_general | solution.py:83
  227.0 2.3 copy.38
  229.3 1.2 copy.39
  230.5 1.2 copy.40
  231.6 0.7 convert_reduce_fusion
  (32 shorter events, 0.5 us)
Async XLA Ops:
  0.6 14.2 %copy-start.3 = (bf16[512,768]{1,0:T(8,128)(2,1)S(1)}, bf16[512,768]{1,0:T(8,128)(2,1)}, u32[]{:S(2)}) copy-start(bf16[512,768]{1,0:T(8,128)(2,1)} %param.10) | copy-start | bytes 2359300
  14.8 117.4 %copy-start.1 = (bf16[2,256,512]{2,1,0:T(8,128)(2,1)}, bf16[2,256,512]{2,1,0:T(8,128)(2,1)S(1)}, u32[]{:S(2)}) copy-start(bf16[2,256,512]{2,1,0:T(8,128)(2,1)S(1)} %all_to_all.35) | copy-start | bytes 1572868
  16.6 10.5 %copy-start.9 = (f32[1536]{0:T(1024)S(1)}, f32[1536]{0:T(1024)}, u32[]{:S(2)}) copy-start(f32[1536]{0:T(1024)} %param.12) | copy-start | bytes 18436
  16.6 49.0 %all-to-all-start.1 = ((f32[16,32,768]{2,1,0:T(8,128)}), f32[16,32,768]{2,1,0:T(8,128)S(1)}, u32[]{:S(2)}, u32[]{:S(2)}) async-start(f32[16,32,768]{2,1,0:T(8,128)} %fusion.15), calls=%async_computation.1 | async-start | bytes 3145728 | tf_op jit(solution)/shard_map/all_to_all | solution.py:51
  65.6 27.3 %copy-start.7 = (f32[32,768]{1,0:T(8,128)}, f32[32,768]{1,0:T(8,128)S(1)}, u32[]{:S(2)}) copy-start(f32[32,768]{1,0:T(8,128)S(1)} %reduce_sum.90) | copy-start | bytes 294916
  65.6 27.2 %copy-start = (bf16[768,512]{1,0:T(8,128)(2,1)S(1)}, bf16[768,512]{1,0:T(8,128)(2,1)}, u32[]{:S(2)}) copy-start(bf16[768,512]{1,0:T(8,128)(2,1)} %param.11) | copy-start | bytes 2359300
  113.6 18.6 %copy-start.10 = (f32[512]{0:T(512)S(1)}, f32[512]{0:T(512)}, u32[]{:S(2)}) copy-start(f32[512]{0:T(512)} %param.13) | copy-start | bytes 6148
  133.0 0.8 copy-start.5
  135.6 57.6 %all-to-all-start.5 = ((f32[16,32,768]{2,1,0:T(8,128)}), f32[16,32,768]{2,1,0:T(8,128)S(1)}, u32[]{:S(2)}, u32[]{:S(2)}) async-start(f32[16,32,768]{2,1,0:T(8,128)} %fusion.11), calls=%async_computation.5 | async-start | bytes 3145728 | tf_op jit(solution)/shard_map/all_to_all | solution.py:51
  192.3 1.0 copy-start.8
  193.3 7.0 %copy-start.4 = (bf16[512,768]{1,0:T(8,128)(2,1)S(1)}, bf16[512,768]{1,0:T(8,128)(2,1)}, u32[]{:S(2)}) copy-start(bf16[512,768]{1,0:T(8,128)(2,1)} %param.10) | copy-start | bytes 2359300
  194.3 28.6 %all-to-all-start.6 = ((bf16[16,32,768]{2,1,0:T(8,128)(2,1)}), bf16[16,32,768]{2,1,0:T(8,128)(2,1)S(1)}, u32[]{:S(2)}, u32[]{:S(2)}) async-start(bf16[16,32,768]{2,1,0:T(8,128)(2,1)} %broadcast_in_dim.12), calls=%async_computation.6 | async-start | bytes 1572864 | tf_op jit(solution)/shard_map/all_to_all | solution.py:22
  203.7 2.5 %copy-start.6 = (bf16[16,32,512]{2,1,0:T(8,128)(2,1)S(1)}, bf16[16,32,512]{2,1,0:T(8,128)(2,1)}, u32[]{:S(2)}) copy-start(bf16[16,32,512]{2,1,0:T(8,128)(2,1)} %copy-done.5) | copy-start | bytes 1572868
  206.2 16.7 %copy-start.2 = (bf16[2,256,512]{2,1,0:T(8,128)(2,1)S(1)}, bf16[2,256,512]{2,1,0:T(8,128)(2,1)}, u32[]{:S(2)}) copy-start(bf16[2,256,512]{2,1,0:T(8,128)(2,1)} %copy-done.1) | copy-start | bytes 1572868
where the time goes:
time: 233 us; the launch traced here: 232 us
  blocking collectives  128 us (55%)
  waiting for transfers between devices  50.3 us (22%)
  starting transfers between devices  23 us (10%)
  local copies, waits for them, and re-layouts  13.5 us (6%)
  matrix products  12.9 us (6%)
  other arithmetic  3.77 us (2%)
    all_to_all x3, blocking collectives, sent_to_all(): lax.all_to_all(jnp.broadcast_to(array[None], (peers, *array.shape)), axis...  58.7 us
    all_gather x1, blocking collectives, total_of_pieces(): parts = lax.all_gather(array, axis)  49.2 us
    all_to_all x2, waiting for transfers between devices, sent_and_summed(): parts = lax.all_to_all(in_blocks(array, dim, peers), axis, 0, 0, tiled=True)  38.4 us
    all_to_all x1, blocking collectives, sent_and_summed(): parts = lax.all_to_all(in_blocks(array, dim, peers), axis, 0, 0, tiled=True)  20.1 us
    all_to_all x2, starting transfers between devices, sent_and_summed(): parts = lax.all_to_all(in_blocks(array, dim, peers), axis, 0, 0, tiled=True)  17.1 us
    all_to_all x1, waiting for transfers between devices, sent_to_all(): lax.all_to_all(jnp.broadcast_to(array[None], (peers, *array.shape)), axis...  12 us
    unnamed x28, local copies, waits for them, and re-layouts  11.2 us
    dot_general x2, matrix products, contract_rows(): lax.dot_general(left, right, (((0,), (0,)), ((), ())), preferred_element_...  8.84 us
  transfers between devices with their start and end apart: 3, of which 2 were waited for; matrix products, arithmetic and copies ran while one was open for 5% of the time, Pallas kernels for 0%

commit v1 on v0

v1 whole, which is shorter than its diff:
```python
import functools

import jax
import jax.numpy as jnp
from jax import lax
from jax.experimental import pallas as pl
from jax.experimental.pallas import tpu as pltpu
from jax.sharding import PartitionSpec as P

beta_one = 0.9
beta_two = 0.999
learn_rate = 0.001
adam_eps = 1e-08
bias_one = 0.9999734386011124
bias_two = 0.09520785288629115
norm_eps = 1e-06
sparsity = 1.0

MESH = pl.DeviceIdType.MESH
F32 = jnp.float32
BF16 = jnp.bfloat16

CHIPS = 8
SIDE = 4
LANES = 128
FAR_Z = (4, 3, 5, 2, 6, 1, 7)
FAR_XY = tuple(
    sorted(
        ((a, b) for a in range(SIDE) for b in range(SIDE) if a or b),
        key=lambda s: -(min(s[0], SIDE - s[0]) + min(s[1], SIDE - s[1])),
    )
)


def dot_nt(left, right):
    return lax.dot_general(
        left, right, (((1,), (1,)), ((), ())), preferred_element_type=F32
    )


def dot_tn(left, right):
    return lax.dot_general(
        left, right, (((0,), (0,)), ((), ())), preferred_element_type=F32
    )


def dot_nn(left, right):
    return jnp.dot(left, right, preferred_element_type=F32)


def adam_step(weight, moment_one, moment_two, gradient):
    first_next = beta_one * moment_one.astype(F32) + (1.0 - beta_one) * gradient
    second_next = (
        beta_two * moment_two.astype(F32) + (1.0 - beta_two) * gradient * gradient
    )
    stepped = weight.astype(F32) - learn_rate * (first_next / bias_one) / (
        jnp.sqrt(second_next / bias_two) + adam_eps
    )
    return stepped.astype(BF16), first_next.astype(BF16), second_next.astype(BF16)


def exchange_kernel(
    acts_hbm, enc_hbm, dec_hbm, m_hbm, v_hbm, ebias_ref, dbias_ref,
    tok_out, gpre_out, w_out, m_out, v_out, rsum_out,
    tok, enc, dec, lat, grad, gpre,
    keep, give_wide, took_wide, give, took, half, rs_wide, rs_z, pre,
    rb, rb_low, rs_xy,
    sq_lane, norm_lane, sq_col, norm_col,
    m_old, v_old, w_new, m_new, v_new,
    load_sem, store_sem, send_sem, recv_sem,
):
    rows, width = acts_hbm.shape
    latents = enc_hbm.shape[1]
    total_rows = 2 * rows
    side = rows // 2
    piece = side // CHIPS
    xy_piece = total_rows // (SIDE * SIDE)
    lines = latents // LANES

    e, l, r = (lax.axis_index(a) for a in ("expert", "latent", "row"))
    z, c = lax.div(e, 2), lax.rem(e, 2)
    y, x = lax.div(l, 2), 2 * r + lax.rem(l, 2)

    def at_z(step):
        return lax.rem(z + step, CHIPS)

    def z_peer(step):
        return (at_z(step) * 2 + c, l, r)

    def at_xy(dx, dy):
        return lax.rem(x + dx, SIDE), lax.rem(y + dy, SIDE)

    def xy_peer(dx, dy):
        px, py = at_xy(dx, dy)
        return (e, py * 2 + lax.rem(px, 2), lax.div(px, 2))

    pair = (z * 2 + 1 - c, l, r)
    mirror_x = SIDE - 1 - x
    mirror = (e, y * 2 + lax.rem(mirror_x, 2), lax.div(mirror_x, 2))

    count = [0]
    sent = []

    def send(src, dst, to):
        n = count[0]
        count[0] += 1
        copy = pltpu.make_async_remote_copy(
            src_ref=src, dst_ref=dst, send_sem=send_sem.at[n], recv_sem=recv_sem.at[n],
            device_id=to, device_id_type=MESH,
        )
        copy.start()
        sent.append(copy)
        return copy

    def arrived(copies):
        for copy in copies:
            copy.wait_recv()

    def span(start, size):
        return pl.ds(pl.multiple_of(start, size), size)

    own_base, other_base = r * rows, (1 - r) * rows
    own_rows = span(own_base, rows)
    my_piece = c * side + z * piece

    loads = [
        pltpu.make_async_copy(src, dst, load_sem.at[n])
        for n, (src, dst) in enumerate(
            (
                (acts_hbm, tok.at[own_rows]), (enc_hbm, enc), (dec_hbm, dec),
                (m_hbm, m_old), (v_hbm, v_old),
            )
        )
    ]
    barrier = pltpu.get_barrier_semaphore()
    greeted = [*(z_peer(s) for s in FAR_Z), *(xy_peer(*s) for s in FAR_XY), pair]
    for to in greeted:
        pl.semaphore_signal(barrier, inc=1, device_id=to, device_id_type=MESH)
    for load in loads:
        load.start()

    def encode_part(k, base):
        give_wide[k] = dot_nn(tok[span(base + (1 - c) * side, side)], enc[...])
        keep[k] = dot_nn(tok[span(base + c * side, side)], enc[...])

    loads[0].wait()
    loads[1].wait()
    encode_part(0, own_base)
    loads[2].wait()
    wide = dec[...].astype(F32)
    square = wide * wide
    high = square.astype(BF16)
    low = (square - high.astype(F32)).astype(BF16)
    ones_lane = jnp.ones((8, width), BF16)
    ones_col = jnp.ones((width, LANES), BF16)
    lane = dot_nt(ones_lane, high) + dot_nt(ones_lane, low)
    sq_lane[0] = jnp.concatenate(
        [lane[0:1, n * LANES : (n + 1) * LANES] for n in range(lines)]
        + [jnp.zeros((8 - lines, LANES), F32)],
        axis=0,
    )
    sq_col[0] = dot_nn(high, ones_col) + dot_nn(low, ones_col)
    pl.semaphore_wait(barrier, len(greeted))

    acts_copy = send(tok.at[own_rows], tok.at[own_rows], mirror)
    core_a = send(give_wide.at[0], took_wide.at[0], pair)
    lane_copy = send(sq_lane.at[0], sq_lane.at[1], pair)

    def z_scatter(values, slots):
        return [
            send(values.at[span(at_z(s) * piece, piece)], slots.at[s], z_peer(s))
            for s in FAR_Z
        ]

    def z_summed(k, copies, slots):
        arrived(copies)
        total = keep[k, span(z * piece, piece)]
        for s in range(1, CHIPS):
            total = total + slots[s].astype(F32)
        return total

    def z_gather(buf, base):
        at = span(base + my_piece, piece)
        return [send(buf.at[at], buf.at[at], z_peer(s)) for s in FAR_Z]

    def z_forward(buf, base, copies):
        arrived(copies)
        at = span(base + c * side, side)
        return send(buf.at[at], buf.at[at], pair)

    core_a.wait_recv()
    keep[0] = keep[0] + took_wide[0]
    scatter_a = z_scatter(keep.at[0], rs_wide.at[0])
    acts_copy.wait_recv()
    encode_part(1, other_base)
    core_b = send(give_wide.at[1], took_wide.at[1], pair)
    col_copy = send(sq_col.at[0], sq_col.at[1], pair)
    core_b.wait_recv()
    keep[1] = keep[1] + took_wide[1]
    scatter_b = z_scatter(keep.at[1], rs_wide.at[1])

    tok_store = pltpu.make_async_copy(tok, tok_out, store_sem.at[0])
    tok_store.start()
    lane_copy.wait_recv()
    norm_lane[0] = jnp.sqrt(sq_lane[0] + sq_lane[1] + norm_eps)
    norm_copies = [send(norm_lane.at[0], norm_lane.at[s], z_peer(s)) for s in FAR_Z]
    bias = jnp.concatenate(
        [ebias_ref[pl.ds(r * lines + n, 1), :] for n in range(lines)], axis=1
    )
    col_copy.wait_recv()
    norm_col[...] = jnp.sqrt(sq_col[0] + sq_col[1] + norm_eps)

    def encode(k, base, index, copies):
        value = z_summed(k, copies, rs_wide.at[k]) + bias
        pre[index] = value
        lat[span(base + my_piece, piece)] = jnp.maximum(value, 0.0).astype(BF16)
        return z_gather(lat, base)

    gather_a = encode(0, own_base, r, scatter_a)
    gather_b = encode(1, other_base, 1 - r, scatter_b)
    forward_a = z_forward(lat, own_base, gather_a)
    forward_b = z_forward(lat, other_base, gather_b)

    def rebuild(base, core):
        at = span(base + core * side, side)
        part = dot_nn(lat[at], dec[...])
        rb[at] = part
        rb_low[at] = part.astype(BF16)

    rebuild(own_base, c)
    rebuild(other_base, c)
    forward_a.wait_recv()
    rebuild(own_base, 1 - c)
    forward_b.wait_recv()
    rebuild(other_base, 1 - c)

    scatter = []
    for dx, dy in FAR_XY:
        px, py = at_xy(dx, dy)
        at = span((px * SIDE + py) * xy_piece, xy_piece)
        scatter.append(send(rb_low.at[at], rs_xy.at[dx * SIDE + dy], xy_peer(dx, dy)))
    dbias = jnp.concatenate(
        [dbias_ref[n : n + 1, :] for n in range(width // LANES)], axis=1
    )
    arrived(scatter)
    mine = span((x * SIDE + y) * xy_piece, xy_piece)
    total = rb[mine]
    for n in range(1, SIDE * SIDE):
        total = total + rs_xy[n].astype(F32)
    grad_rows = 2.0 * (total + dbias - tok[mine].astype(F32)) / total_rows
    grad[mine] = grad_rows.astype(BF16)
    gather = [send(grad.at[mine], grad.at[mine], xy_peer(*s)) for s in FAR_XY]

    arrived(norm_copies)
    strength = norm_lane[0]
    for s in range(1, CHIPS):
        strength = strength + norm_lane[s]
    strength = (sparsity / total_rows) * strength
    penalty = jnp.concatenate([strength[n : n + 1, :] for n in range(lines)], axis=1)
    arrived(gather)

    def back_start(k, base):
        give[k] = dot_nt(grad[span(base + (1 - c) * side, side)], dec[...]).astype(BF16)
        copy = send(give.at[k], took.at[k], pair)
        keep[k + 2] = dot_nt(grad[span(base + c * side, side)], dec[...])
        return copy

    def back_scatter(k, copy):
        copy.wait_recv()
        total = keep[k + 2] + took[k].astype(F32)
        keep[k + 2] = total
        half[k] = total.astype(BF16)
        return z_scatter(half.at[k], rs_z.at[k])

    core_a = back_start(0, 0)
    core_b = back_start(1, rows)
    scatter_a = back_scatter(0, core_a)
    scatter_b = back_scatter(1, core_b)

    loads[3].wait()
    loads[4].wait()
    ones_rows = jnp.ones((total_rows, LANES), BF16)

    def decoder_block(n, carry):
        at = span(n * LANES, LANES)
        acts = lat[:, at]
        gradient = dot_tn(acts, grad[...])
        factor = (sparsity / total_rows) * dot_tn(acts, ones_rows) / norm_col[at]
        weight = dec[at]
        gradient = gradient + jnp.tile(factor, (1, width // LANES)) * weight.astype(F32)
        w_new[at], m_new[at], v_new[at] = adam_step(weight, m_old[at], v_old[at], gradient)
        return carry

    lax.fori_loop(0, lines, decoder_block, 0)
    stores = [
        tok_store,
        pltpu.make_async_copy(w_new, w_out, store_sem.at[1]),
        pltpu.make_async_copy(m_new, m_out, store_sem.at[2]),
        pltpu.make_async_copy(v_new, v_out, store_sem.at[3]),
    ]
    for store in stores[1:]:
        store.start()

    def back(k, base, copies):
        value = z_summed(k + 2, copies, rs_z.at[k]) + penalty
        value = jnp.where(pre[k] > 0, value, 0.0)
        gpre[span(base + my_piece, piece)] = value.astype(BF16)
        return z_gather(gpre, base)

    gather_a = back(0, 0, scatter_a)
    gather_b = back(1, rows, scatter_b)
    row_sum = dot_nn(jnp.ones((8, total_rows), BF16), grad[...])
    rsum_out[...] = jnp.concatenate(
        [row_sum[0:1, n * LANES : (n + 1) * LANES] for n in range(width // LANES)], axis=0
    )
    forward_a = z_forward(gpre, 0, gather_a)
    forward_b = z_forward(gpre, rows, gather_b)
    forward_a.wait_recv()
    forward_b.wait_recv()
    stores.append(pltpu.make_async_copy(gpre, gpre_out, store_sem.at[4]))
    stores[-1].start()
    for copy in sent:
        copy.wait_send()
    for store in stores:
        store.wait()


def exchange(acts, enc_weight, dec_weight, dec_first, dec_second, enc_bias, dec_bias):
    rows, width = acts.shape
    latents = enc_weight.shape[1]
    total_rows = 2 * rows
    side = rows // 2
    piece = side // CHIPS
    xy_piece = total_rows // (SIDE * SIDE)
    sems = 104
    hbm = pl.BlockSpec(memory_space=pltpu.HBM)
    vmem = pl.BlockSpec(memory_space=pltpu.VMEM)
    dec_shape = (latents, width)
    return pl.pallas_call(
        exchange_kernel,
        name="exchange",
        out_shape=(
            jax.ShapeDtypeStruct((total_rows, width), BF16),
            jax.ShapeDtypeStruct((total_rows, latents), BF16),
            jax.ShapeDtypeStruct(dec_shape, BF16),
            jax.ShapeDtypeStruct(dec_shape, BF16),
            jax.ShapeDtypeStruct(dec_shape, BF16),
            jax.ShapeDtypeStruct((width // LANES, LANES), F32),
        ),
        in_specs=[hbm] * 5 + [vmem] * 2,
        out_specs=(hbm,) * 5 + (vmem,),
        scratch_shapes=[
            pltpu.VMEM((total_rows, width), BF16),
            pltpu.VMEM((width, latents), BF16),
            pltpu.VMEM(dec_shape, BF16),
            pltpu.VMEM((total_rows, latents), BF16),
            pltpu.VMEM((total_rows, width), BF16),
            pltpu.VMEM((total_rows, latents), BF16),
            pltpu.VMEM((4, side, latents), F32),
            pltpu.VMEM((2, side, latents), F32),
            pltpu.VMEM((2, side, latents), F32),
            pltpu.VMEM((2, side, latents), BF16),
            pltpu.VMEM((2, side, latents), BF16),
            pltpu.VMEM((2, side, latents), BF16),
            pltpu.VMEM((2, CHIPS, piece, latents), F32),
            pltpu.VMEM((2, CHIPS, piece, latents), BF16),
            pltpu.VMEM((2, piece, latents), F32),
            pltpu.VMEM((total_rows, width), F32),
            pltpu.VMEM((total_rows, width), BF16),
            pltpu.VMEM((SIDE * SIDE, xy_piece, width), BF16),
            pltpu.VMEM((2, 8, LANES), F32),
            pltpu.VMEM((CHIPS, 8, LANES), F32),
            pltpu.VMEM((2, latents, LANES), F32),
            pltpu.VMEM((latents, LANES), F32),
            *[pltpu.VMEM(dec_shape, BF16)] * 5,
            pltpu.SemaphoreType.DMA((5,)),
            pltpu.SemaphoreType.DMA((5,)),
            pltpu.SemaphoreType.DMA((sems,)),
            pltpu.SemaphoreType.DMA((sems,)),
        ],
        compiler_params=pltpu.CompilerParams(
            collective_id=0, has_side_effects=True, vmem_limit_bytes=60 << 20
        ),
    )(acts, enc_weight, dec_weight, dec_first, dec_second, enc_bias, dec_bias)


def finish_kernel(
    tok_ref, gpre_ref, w, m, v, rsum_ref, w_done, m_done, v_done,
    w_next, m_next, v_next, bsum_out, rsum_out, w_out, m_out, v_out,
):
    @pl.when(pl.program_id(0) == 0)
    def _():
        total = dot_nn(jnp.ones((8, gpre_ref.shape[0]), BF16), gpre_ref[...])
        for n in range(bsum_out.shape[0]):
            bsum_out[n : n + 1, :] = total[0:1, n * LANES : (n + 1) * LANES]
        rsum_out[...] = rsum_ref[...]

    gradient = dot_tn(tok_ref[...], gpre_ref[...])
    w_next[...], m_next[...], v_next[...] = adam_step(w[...], m[...], v[...], gradient)
    w_out[...] = w_done[...]
    m_out[...] = m_done[...]
    v_out[...] = v_done[...]


def finish(tok, gpre, w, m, v, row_sum, decoder, blocks=4):
    total_rows, latents = gpre.shape
    width = w.shape[0]
    block = pl.BlockSpec((width // blocks, latents), lambda i: (i, 0))
    turned = pl.BlockSpec((latents // blocks, width), lambda i: (i, 0))

    def whole(shape):
        return pl.BlockSpec(shape, lambda i: (0, 0))

    shapes = (latents // LANES, LANES), (width // LANES, LANES)
    return pl.pallas_call(
        finish_kernel,
        name="finish",
        grid=(blocks,),
        out_shape=(jax.ShapeDtypeStruct(w.shape, BF16),) * 3
        + tuple(jax.ShapeDtypeStruct(s, F32) for s in shapes)
        + (jax.ShapeDtypeStruct(decoder[0].shape, BF16),) * 3,
        in_specs=[
            pl.BlockSpec((total_rows, width // blocks), lambda i: (0, i)),
            whole((total_rows, latents)), block, block, block, whole(shapes[1]),
            turned, turned, turned,
        ],
        out_specs=(block,) * 3 + tuple(whole(s) for s in shapes) + (turned,) * 3,
        compiler_params=pltpu.CompilerParams(vmem_limit_bytes=56 << 20),
    )(tok, gpre, w, m, v, row_sum, *decoder)


def local(
    model_acts, enc_weight, dec_weight, enc_bias, dec_bias,
    enc_first, enc_second, dec_first, dec_second,
):
    tok, gpre, *decoder, row_sum = exchange(
        model_acts, enc_weight, dec_weight, dec_first, dec_second,
        enc_bias.reshape(-1, LANES), dec_bias.reshape(-1, LANES),
    )
    encoder = finish(tok, gpre, enc_weight, enc_first, enc_second, row_sum, decoder)
    enc_next, enc_m, enc_v, bias_sum, row_sum, dec_next, dec_m, dec_v = encoder
    return (
        enc_next, dec_next, enc_m, enc_v, dec_m, dec_v,
        bias_sum.reshape(-1), row_sum.reshape(-1),
    )


def solution(mesh):
    split = P("expert", ("latent", "row"))
    turned = P(("latent", "row"), "expert")
    return jax.shard_map(
        local,
        mesh=mesh,
        in_specs=(
            P("row", "expert"), split, turned, P("latent"), P("expert"),
            split, split, turned, turned,
        ),
        out_specs=(
            split, turned, split, split, turned, turned,
            P(("latent", "row")), P("expert"),
        ),
        check_vma=False,
    )
```

time: 233 us -> 93.2 us (0.40)
  blocking collectives: 128 us -> 0 us
  Pallas kernels: 0 us -> 92.3 us
  waiting for transfers between devices: 50.3 us -> 0 us
  starting transfers between devices: 23 us -> 0 us
  local copies, waits for them, and re-layouts: 13.5 us -> 0 us
  matrix products: 12.9 us -> 0 us
  other arithmetic: 3.77 us -> 0 us
    pallas_call x0 -> x2, Pallas kernels: none -> 92.3 us  [the longest x1 85.4 us: exchange(): pl.pallas_call(exchange_kernel, name='exchange', out_shape=(jax.ShapeDtyp...]
    all_to_all x4 -> x0, blocking collectives: 78.8 us -> none  [the longest x3 58.7 us: sent_to_all(): lax.all_to_all(jnp.broadcast_to(array[None], (peers, *array.shape)), axis...]
    all_to_all x3 -> x0, waiting for transfers between devices: 50.3 us -> none  [the longest x2 38.4 us: sent_and_summed(): parts = lax.all_to_all(in_blocks(array, dim, peers), axis, 0, 0, tiled=True)]
    all_gather x1 -> x0, blocking collectives: 49.2 us -> none  [total_of_pieces(): parts = lax.all_gather(array, axis)]
    all_to_all x3 -> x0, starting transfers between devices: 23 us -> none  [the longest x2 17.1 us: sent_and_summed(): parts = lax.all_to_all(in_blocks(array, dim, peers), axis, 0, 0, tiled=True)]
    dot_general x5 -> x0, matrix products: 12.9 us -> none  [the longest x2 8.84 us: contract_rows(): lax.dot_general(left, right, (((0,), (0,)), ((), ())), preferred_element_...]
    unnamed x28 -> x0, local copies, waits for them, and re-layouts: 11.2 us -> none
    reduce_sum x9 -> x0, other arithmetic: 3.66 us -> none  [the longest x1 0.85 us: local(): own_norm = jnp.sum(decoder_norms * column_pick[None, :], axis=1)]
  transfers between devices with their start and end apart: 3 -> 0, of which waited for: 2 -> 0; matrix products, arithmetic and copies ran while one was open for 5% -> 0% of each run, Pallas kernels for 0% -> 0%
where the time goes in v1:
time: 93.2 us; the launch traced here: 93 us
  Pallas kernels  92.3 us (99%)
    pallas_call x1, Pallas kernels, exchange(): pl.pallas_call(exchange_kernel, name='exchange', out_shape=(jax.ShapeDtyp...  85.4 us
    pallas_call x1, Pallas kernels, finish(): pl.pallas_call(finish_kernel, name='finish', grid=(blocks,), out_shape=(j...  6.91 us

profile of v1, /device:TPU:1, one launch (start us, length us, event | category | flops | bytes accessed | tf_op | source)
XLA Modules:
  0.0 93.0 jit_solution(781446074378640838)
XLA Ops:
  0.6 85.4 %exchange.1 = (bf16[512,512]{1,0:T(8,128)(2,1)}, bf16[512,768]{1,0:T(8,128)(2,1)}, bf16[768,512]{1,0:T(8,128)(2,1)}, bf16[768,512]{1,0:T(8,128)(2,1)}, bf16[768,512]{1,0:T(8,128)(2,1)}, /*index=5*/f32[4,128]{1,0:T(4,128)}) custom-call(bf16[256,512]{1,0:T(8,128)(2,1)} %acts_hbm.1, bf16[512,768]{1,0:T(8,128)(2,1)} %w.1, bf16[768,512]{1,0:T(8,128)(2,1)} %dec_hbm.1, ...), custom_call_target="tpu_custom_call" | custom-call | tf_op jit(solution)/shard_map/exchange/pallas_call | solution.py:339
  86.1 6.9 %finish.1 = (bf16[512,768]{1,0:T(8,128)(2,1)}, bf16[512,768]{1,0:T(8,128)(2,1)}, bf16[512,768]{1,0:T(8,128)(2,1)}, f32[6,128]{1,0:T(8,128)}, f32[4,128]{1,0:T(4,...) custom-call(bf16[512,512]{1,0:T(8,128)(2,1)} %get-tuple-element.22.tok_ref, ...), custom_call_target="tpu_custom_call" | custom-call | tf_op jit(solution)/shard_map/finish/pallas_call | solution.py:415

commit v2 on v1

v2 whole, which is shorter than its diff:
```python
import functools

import jax
import jax.numpy as jnp
from jax import lax
from jax.experimental import pallas as pl
from jax.experimental.pallas import tpu as pltpu
from jax.sharding import PartitionSpec as P

beta_one = 0.9
beta_two = 0.999
learn_rate = 0.001
adam_eps = 1e-08
bias_one = 0.9999734386011124
bias_two = 0.09520785288629115
norm_eps = 1e-06
sparsity = 1.0

MESH = pl.DeviceIdType.MESH
F32 = jnp.float32
BF16 = jnp.bfloat16

CHIPS = 8
SIDE = 4
LANES = 128
SENDS = 136
FAR_Z = (4, 3, 5, 2, 6, 1, 7)
FAR_XY = tuple(
    sorted(
        ((a, b) for a in range(SIDE) for b in range(SIDE) if a or b),
        key=lambda s: -(min(s[0], SIDE - s[0]) + min(s[1], SIDE - s[1])),
    )
)


def dot_nt(left, right):
    return lax.dot_general(
        left, right, (((1,), (1,)), ((), ())), preferred_element_type=F32
    )


def dot_tn(left, right):
    return lax.dot_general(
        left, right, (((0,), (0,)), ((), ())), preferred_element_type=F32
    )


def dot_nn(left, right):
    return jnp.dot(left, right, preferred_element_type=F32)


def adam_step(weight, moment_one, moment_two, gradient):
    first_next = beta_one * moment_one.astype(F32) + (1.0 - beta_one) * gradient
    second_next = beta_two * moment_two.astype(F32) + (1.0 - beta_two) * (gradient * gradient)
    root = bias_two**0.5
    move = (learn_rate * root / bias_one) * first_next / (jnp.sqrt(second_next) + adam_eps * root)
    stepped = weight.astype(F32) - move
    return stepped.astype(BF16), first_next.astype(BF16), second_next.astype(BF16)


def exchange_kernel(
    acts_hbm, enc_hbm, dec_hbm, m_hbm, v_hbm, ebias_ref, dbias_ref,
    tok_out, gpre_out, w_out, m_out, v_out, rsum_out,
    tok, enc, dec, dbias, lat, gside, grad, gpre,
    keep, half, rs_wide, relay, rs_z, pre,
    rb, rb_low, rs_xy, norm_lane, norm_col,
    m_old, v_old, w_new, m_new, v_new,
    load_sem, store_sem, send_sem, recv_sem,
):
    rows, width = acts_hbm.shape
    latents = enc_hbm.shape[1]
    total_rows = 2 * rows
    side = rows // 2
    piece = side // CHIPS
    lines = latents // LANES
    row_scale = sparsity / total_rows

    e, l, r = (lax.axis_index(a) for a in ("expert", "latent", "row"))
    z, c = lax.div(e, 2), lax.rem(e, 2)
    y, x = lax.div(l, 2), 2 * r + lax.rem(l, 2)

    def at_z(step):
        return lax.rem(z + step + CHIPS, CHIPS)

    def z_peer(step):
        return (at_z(step) * 2 + c, l, r)

    def at_xy(dx, dy):
        return lax.rem(x + dx, SIDE), lax.rem(y + dy, SIDE)

    def xy_peer(dx, dy):
        px, py = at_xy(dx, dy)
        return (e, py * 2 + lax.rem(px, 2), lax.div(px, 2))

    mirror_x = SIDE - 1 - x
    mirror_l, mirror_r = y * 2 + lax.rem(mirror_x, 2), lax.div(mirror_x, 2)
    other = z * 2 + 1 - c
    pair = (other, l, r)
    mirror, mirror_pair = (e, mirror_l, mirror_r), (other, mirror_l, mirror_r)

    count = [0]
    sent = []

    def send(src, dst, to):
        n = count[0]
        count[0] += 1
        copy = pltpu.make_async_remote_copy(
            src_ref=src, dst_ref=dst, send_sem=send_sem.at[n], recv_sem=recv_sem.at[n],
            device_id=to, device_id_type=MESH,
        )
        copy.start()
        sent.append(copy)
        return copy

    def arrived(copies):
        for copy in copies:
            copy.wait_recv()

    def span(start, size):
        return pl.ds(pl.multiple_of(start, size), size)

    def side_rows(h, core):
        return span(h * rows + core * side, side)

    def own_piece(h):
        return span(h * rows + c * side + z * piece, piece)

    loads = [
        pltpu.make_async_copy(src, dst, load_sem.at[n])
        for n, (src, dst) in enumerate(
            (
                (acts_hbm, tok.at[0, span(r * rows, rows)]),
                (enc_hbm, enc.at[0]), (dec_hbm, dec.at[0]),
                (m_hbm, m_old), (v_hbm, v_old),
            )
        )
    ]
    barrier = pltpu.get_barrier_semaphore()
    greeted = [
        *(z_peer(s) for s in FAR_Z), *(xy_peer(*s) for s in FAR_XY), mirror_pair, pair
    ]
    for to in greeted:
        pl.semaphore_signal(barrier, inc=1, device_id=to, device_id_type=MESH)
    for load in loads:
        load.start()
    loads[0].wait()
    loads[1].wait()
    keep[0] = dot_nn(tok[0, side_rows(r, c)], enc[0])
    dbias[0] = jnp.concatenate(
        [dbias_ref[n : n + 1, :] for n in range(width // LANES)], axis=1
    )
    loads[2].wait()
    pl.semaphore_wait(barrier, len(greeted))

    give, mine = side_rows(r, 1 - c), side_rows(r, c)
    acts_pair = send(tok.at[0, give], tok.at[1, give], pair)
    enc_pair = send(enc.at[0], enc.at[1], pair)
    acts_far = [
        send(tok.at[0, mine], tok.at[0, mine], mirror),
        send(tok.at[0, give], tok.at[1, give], mirror_pair),
    ]
    dec_pair = send(dec.at[0], dec.at[1], pair)
    bias_pair = send(dbias.at[0], dbias.at[1], pair)

    def z_part(values, step):
        return values.at[span(at_z(step) * piece, piece)]

    def z_scatter(values, slots):
        return [send(z_part(values, s), slots.at[s], z_peer(s)) for s in FAR_Z]

    def relay_start(values, slots, s):
        return [
            send(z_part(values, n), slots.at[i], z_peer(to))
            for i, (n, to) in enumerate(
                ((4 * s, -2 * s), (-3 * s, -s), (3 * s, s), (-s, -s), (s, s))
            )
        ]

    def relay_pass(values, slots, hold, copies, s):
        arrived(copies[:2])
        hold[0] = z_part(values, -2 * s)[...] + slots[0] + slots[1]
        back = send(hold.at[0], slots.at[5], z_peer(-2 * s))
        arrived(copies[2:3])
        hold[1] = z_part(values, 2 * s)[...] + slots[2]
        return [*copies[3:], back, send(hold.at[1], slots.at[6], z_peer(2 * s))]

    def z_gather(buf, h):
        at = own_piece(h)
        return [send(buf.at[at], buf.at[at], z_peer(s)) for s in FAR_Z]

    arrived([acts_pair, enc_pair])
    keep[0] = keep[0] + dot_nn(tok[1, mine], enc[1])
    first = relay_start(keep.at[0], rs_wide.at[0], 1)
    arrived(acts_far)
    theirs = side_rows(1 - r, c)
    keep[1] = dot_nn(tok[0, theirs], enc[0]) + dot_nn(tok[1, theirs], enc[1])
    second = relay_start(keep.at[1], rs_wide.at[1], -1)
    first = relay_pass(keep.at[0], rs_wide.at[0], relay.at[0], first, 1)
    second = relay_pass(keep.at[1], rs_wide.at[1], relay.at[1], second, -1)
    acts_back = send(tok.at[1, theirs], tok.at[0, theirs], pair)

    ones_lane = jnp.ones((8, width), BF16)
    ones_col = jnp.ones((width, LANES), BF16)
    arrived([dec_pair, bias_pair])
    lane, column = norm_eps, norm_eps
    for f in range(2):
        wide = dec[f].astype(F32)
        square = wide * wide
        high = square.astype(BF16)
        low = (square - high.astype(F32)).astype(BF16)
        lane = lane + (dot_nt(ones_lane, high) + dot_nt(ones_lane, low))
        column = column + (dot_nn(high, ones_col) + dot_nn(low, ones_col))
    norm_col[...] = jnp.sqrt(column)
    norm_lane[0] = jnp.sqrt(
        jnp.concatenate(
            [lane[0:1, n * LANES : (n + 1) * LANES] for n in range(lines)]
            + [jnp.zeros((8 - lines, LANES), F32)],
            axis=0,
        )
    )
    norm_copies = [send(norm_lane.at[0], norm_lane.at[s], z_peer(s)) for s in FAR_Z]
    bias = jnp.concatenate(
        [ebias_ref[pl.ds(r * lines + n, 1), :] for n in range(lines)], axis=1
    )

    def encode(k, h, copies):
        arrived(copies)
        value = keep[k, span(z * piece, piece)] + bias
        for n in range(3, 7):
            value = value + rs_wide[k, n]
        pre[h] = value
        lat[own_piece(h)] = jnp.maximum(value, 0.0).astype(BF16)
        return z_gather(lat, h)

    first = encode(0, r, first)
    second = encode(1, 1 - r, second)

    def rebuild(f, h):
        at = span(h * side, side)
        part = dot_nn(lat[side_rows(h, c)], dec[f])
        rb[f, at] = part
        rb_low[f, at] = part.astype(BF16)

    def plane_scatter(f):
        copies = []
        for dx, dy in FAR_XY:
            px, py = at_xy(dx, dy)
            at = span((px * SIDE + py) * piece, piece)
            copies.append(
                send(rb_low.at[f, at], rs_xy.at[f, dx * SIDE + dy], xy_peer(dx, dy))
            )
        return copies

    arrived(first)
    rebuild(0, r)
    arrived(second)
    rebuild(0, 1 - r)
    scatter_own = plane_scatter(0)
    rebuild(1, r)
    rebuild(1, 1 - r)
    scatter_pair = plane_scatter(1)
    lat_copies = [
        send(lat.at[side_rows(h, c)], lat.at[side_rows(h, c)], pair) for h in range(2)
    ]

    place = x * SIDE + y
    at_place = span(place * piece, piece)
    from_rows = lax.div(place, CHIPS) * rows + c * side + lax.rem(place, CHIPS) * piece

    def residual(f, copies):
        arrived(copies)
        total = rb[f, at_place]
        for n in range(1, SIDE * SIDE):
            total = total + rs_xy[f, n].astype(F32)
        acts = tok[f, span(from_rows, piece)].astype(F32)
        grad_rows = 2.0 * (total + dbias[f] - acts) / total_rows
        gside[f, at_place] = grad_rows.astype(BF16)
        ref = gside.at[f, at_place]
        return [send(ref, ref, xy_peer(*s)) for s in FAR_XY]

    gather_own = residual(0, scatter_own)
    gather_pair = residual(1, scatter_pair)
    arrived(norm_copies)
    strength = norm_lane[0]
    for s in range(1, CHIPS):
        strength = strength + norm_lane[s]
    strength = row_scale * strength
    penalty = jnp.concatenate([strength[n : n + 1, :] for n in range(lines)], axis=1)
    arrived([acts_back])
    stores = [pltpu.make_async_copy(tok.at[0], tok_out, store_sem.at[0])]
    stores[0].start()

    arrived(gather_own)
    for h in range(2):
        keep[2 + h] = dot_nt(gside[0, h * side : (h + 1) * side], dec[0])
    arrived(gather_pair)
    scatters = []
    for h in range(2):
        total = keep[2 + h] + dot_nt(gside[1, h * side : (h + 1) * side], dec[1])
        keep[2 + h] = total
        half[h] = total.astype(BF16)
        scatters.append(z_scatter(half.at[h], rs_z.at[h]))

    grad_copies = [
        send(gside.at[1, span(h * side, side)], grad.at[side_rows(h, c)], pair)
        for h in range(2)
    ]
    for h in range(2):
        grad[side_rows(h, c)] = gside[0, h * side : (h + 1) * side]
    loads[3].wait()
    loads[4].wait()
    arrived(lat_copies)
    arrived(grad_copies)
    ones_rows = jnp.ones((total_rows, LANES), BF16)

    def decoder_block(n, carry):
        at = span(n * LANES, LANES)
        acts = lat[:, at]
        gradient = dot_tn(acts, grad[...])
        factor = row_scale * dot_tn(acts, ones_rows) / norm_col[at]
        weight = dec[0, at]
        gradient = gradient + jnp.tile(factor, (1, width // LANES)) * weight.astype(F32)
        w_new[at], m_new[at], v_new[at] = adam_step(weight, m_old[at], v_old[at], gradient)
        return carry

    lax.fori_loop(0, lines // 2, decoder_block, 0)

    def back(h, copies):
        arrived(copies)
        value = keep[2 + h, span(z * piece, piece)] + penalty
        for s in range(1, CHIPS):
            value = value + rs_z[h, s].astype(F32)
        gpre[own_piece(h)] = jnp.where(pre[h] > 0, value, 0.0).astype(BF16)
        return z_gather(gpre, h)

    gathers = [back(h, scatters[h]) for h in range(2)]
    lax.fori_loop(lines // 2, lines, decoder_block, 0)
    stores += [
        pltpu.make_async_copy(w_new, w_out, store_sem.at[1]),
        pltpu.make_async_copy(m_new, m_out, store_sem.at[2]),
        pltpu.make_async_copy(v_new, v_out, store_sem.at[3]),
    ]
    for store in stores[1:]:
        store.start()
    row_sum = dot_nn(jnp.ones((8, total_rows), BF16), grad[...])
    rsum_out[...] = jnp.concatenate(
        [row_sum[0:1, n * LANES : (n + 1) * LANES] for n in range(width // LANES)], axis=0
    )
    last = []
    for h in range(2):
        arrived(gathers[h])
        ref = gpre.at[side_rows(h, c)]
        last.append(send(ref, ref, pair))
    arrived(last)
    stores.append(pltpu.make_async_copy(gpre, gpre_out, store_sem.at[4]))
    stores[-1].start()
    for copy in sent:
        copy.wait_send()
    for store in stores:
        store.wait()
    assert count[0] == SENDS


def exchange(acts, enc_weight, dec_weight, dec_first, dec_second, enc_bias, dec_bias):
    rows, width = acts.shape
    latents = enc_weight.shape[1]
    total_rows = 2 * rows
    side = rows // 2
    piece = side // CHIPS
    hbm = pl.BlockSpec(memory_space=pltpu.HBM)
    vmem = pl.BlockSpec(memory_space=pltpu.VMEM)
    dec_shape = (latents, width)
    return pl.pallas_call(
        exchange_kernel,
        name="exchange",
        out_shape=(
            jax.ShapeDtypeStruct((total_rows, width), BF16),
            jax.ShapeDtypeStruct((total_rows, latents), BF16),
            jax.ShapeDtypeStruct(dec_shape, BF16),
            jax.ShapeDtypeStruct(dec_shape, BF16),
            jax.ShapeDtypeStruct(dec_shape, BF16),
            jax.ShapeDtypeStruct((width // LANES, LANES), F32),
        ),
        in_specs=[hbm] * 5 + [vmem] * 2,
        out_specs=(hbm,) * 5 + (vmem,),
        scratch_shapes=[
            pltpu.VMEM((2, total_rows, width), BF16),
            pltpu.VMEM((2, width, latents), BF16),
            pltpu.VMEM((2, *dec_shape), BF16),
            pltpu.VMEM((2, 1, width), F32),
            pltpu.VMEM((total_rows, latents), BF16),
            pltpu.VMEM((2, rows, width), BF16),
            pltpu.VMEM((total_rows, width), BF16),
            pltpu.VMEM((total_rows, latents), BF16),
            pltpu.VMEM((4, side, latents), F32),
            pltpu.VMEM((2, side, latents), BF16),
            pltpu.VMEM((2, 7, piece, latents), F32),
            pltpu.VMEM((2, 2, piece, latents), F32),
            pltpu.VMEM((2, CHIPS, piece, latents), BF16),
            pltpu.VMEM((2, piece, latents), F32),
            pltpu.VMEM((2, rows, width), F32),
            pltpu.VMEM((2, rows, width), BF16),
            pltpu.VMEM((2, SIDE * SIDE, piece, width), BF16),
            pltpu.VMEM((CHIPS, 8, LANES), F32),
            pltpu.VMEM((latents, LANES), F32),
            *[pltpu.VMEM(dec_shape, BF16)] * 5,
            pltpu.SemaphoreType.DMA((5,)),
            pltpu.SemaphoreType.DMA((5,)),
            pltpu.SemaphoreType.DMA((SENDS,)),
            pltpu.SemaphoreType.DMA((SENDS,)),
        ],
        compiler_params=pltpu.CompilerParams(
            collective_id=0, has_side_effects=True, vmem_limit_bytes=60 << 20
        ),
    )(acts, enc_weight, dec_weight, dec_first, dec_second, enc_bias, dec_bias)


def finish_kernel(
    tok_ref, gpre_ref, w, m, v, rsum_ref, w_done, m_done, v_done,
    w_next, m_next, v_next, bsum_out, rsum_out, w_out, m_out, v_out,
):
    @pl.when(pl.program_id(0) == 0)
    def _():
        total = dot_nn(jnp.ones((8, gpre_ref.shape[0]), BF16), gpre_ref[...])
        for n in range(bsum_out.shape[0]):
            bsum_out[n : n + 1, :] = total[0:1, n * LANES : (n + 1) * LANES]
        rsum_out[...] = rsum_ref[...]

    gradient = dot_tn(tok_ref[...], gpre_ref[...])
    w_next[...], m_next[...], v_next[...] = adam_step(w[...], m[...], v[...], gradient)
    w_out[...] = w_done[...]
    m_out[...] = m_done[...]
    v_out[...] = v_done[...]


def finish(tok, gpre, w, m, v, row_sum, decoder, blocks=4):
    total_rows, latents = gpre.shape
    width = w.shape[0]
    block = pl.BlockSpec((width // blocks, latents), lambda i: (i, 0))
    turned = pl.BlockSpec((latents // blocks, width), lambda i: (i, 0))

    def whole(shape):
        return pl.BlockSpec(shape, lambda i: (0, 0))

    shapes = (latents // LANES, LANES), (width // LANES, LANES)
    return pl.pallas_call(
        finish_kernel,
        name="finish",
        grid=(blocks,),
        out_shape=(jax.ShapeDtypeStruct(w.shape, BF16),) * 3
        + tuple(jax.ShapeDtypeStruct(s, F32) for s in shapes)
        + (jax.ShapeDtypeStruct(decoder[0].shape, BF16),) * 3,
        in_specs=[
            pl.BlockSpec((total_rows, width // blocks), lambda i: (0, i)),
            whole((total_rows, latents)), block, block, block, whole(shapes[1]),
            turned, turned, turned,
        ],
        out_specs=(block,) * 3 + tuple(whole(s) for s in shapes) + (turned,) * 3,
        compiler_params=pltpu.CompilerParams(vmem_limit_bytes=56 << 20),
    )(tok, gpre, w, m, v, row_sum, *decoder)


def local(
    model_acts, enc_weight, dec_weight, enc_bias, dec_bias,
    enc_first, enc_second, dec_first, dec_second,
):
    tok, gpre, *decoder, row_sum = exchange(
        model_acts, enc_weight, dec_weight, dec_first, dec_second,
        enc_bias.reshape(-1, LANES), dec_bias.reshape(-1, LANES),
    )
    encoder = finish(tok, gpre, enc_weight, enc_first, enc_second, row_sum, decoder)
    enc_next, enc_m, enc_v, bias_sum, row_sum, dec_next, dec_m, dec_v = encoder
    return (
        enc_next, dec_next, enc_m, enc_v, dec_m, dec_v,
        bias_sum.reshape(-1), row_sum.reshape(-1),
    )


def solution(mesh):
    split = P("expert", ("latent", "row"))
    turned = P(("latent", "row"), "expert")
    return jax.shard_map(
        local,
        mesh=mesh,
        in_specs=(
            P("row", "expert"), split, turned, P("latent"), P("expert"),
            split, split, turned, turned,
        ),
        out_specs=(
            split, turned, split, split, turned, turned,
            P(("latent", "row")), P("expert"),
        ),
        check_vma=False,
    )
```

time: 93.2 us -> 86 us (0.923)
  Pallas kernels: 92.3 us -> 85.2 us
    pallas_call x1, Pallas kernels: 85.4 us -> 78.3 us  [exchange(): pl.pallas_call(exchange_kernel, name='exchange', out_shape=(jax.ShapeDtyp...]
where the time goes in v2:
time: 86 us; the launch traced here: 85.8 us
  Pallas kernels  85.2 us (99%)
    pallas_call x1, Pallas kernels, exchange(): pl.pallas_call(exchange_kernel, name='exchange', out_shape=(jax.ShapeDtyp...  78.3 us
    pallas_call x1, Pallas kernels, finish(): pl.pallas_call(finish_kernel, name='finish', grid=(blocks,), out_shape=(j...  6.84 us

profile of v2, /device:TPU:1, one launch (start us, length us, event | category | flops | bytes accessed | tf_op | source)
XLA Modules:
  0.0 85.8 jit_solution(16002570566019979319)
XLA Ops:
  0.6 78.3 %exchange.1 = (bf16[512,512]{1,0:T(8,128)(2,1)}, bf16[512,768]{1,0:T(8,128)(2,1)}, bf16[768,512]{1,0:T(8,128)(2,1)}, bf16[768,512]{1,0:T(8,128)(2,1)}, bf16[768,512]{1,0:T(8,128)(2,1)}, /*index=5*/f32[4,128]{1,0:T(4,128)}) custom-call(bf16[256,512]{1,0:T(8,128)(2,1)} %acts_hbm.1, bf16[512,768]{1,0:T(8,128)(2,1)} %w.1, bf16[768,512]{1,0:T(8,128)(2,1)} %dec_hbm.1, ...), custom_call_target="tpu_custom_call" | custom-call | tf_op jit(solution)/shard_map/exchange/pallas_call | solution.py:373
  79.0 6.8 %finish.1 = (bf16[512,768]{1,0:T(8,128)(2,1)}, bf16[512,768]{1,0:T(8,128)(2,1)}, bf16[512,768]{1,0:T(8,128)(2,1)}, f32[6,128]{1,0:T(8,128)}, f32[4,128]{1,0:T(4,...) custom-call(bf16[512,512]{1,0:T(8,128)(2,1)} %get-tuple-element.22.tok_ref, ...), custom_call_target="tpu_custom_call" | custom-call | tf_op jit(solution)/shard_map/finish/pallas_call | solution.py:446

commit v3 on v2

--- a/solution.py
+++ b/solution.py
@@ -59,13 +59,13 @@
 
 
 def exchange_kernel(
-    acts_hbm, enc_hbm, dec_hbm, m_hbm, v_hbm, ebias_ref, dbias_ref,
-    tok_out, gpre_out, w_out, m_out, v_out, rsum_out,
+    acts_hbm, enc_hbm, dec_hbm, dec_m_hbm, dec_v_hbm, enc_m_hbm, enc_v_hbm,
+    ebias_hbm, dbias_hbm,
+    tok_out, gpre_out, w_new, m_new, v_new, enc_out, enc_m_out, enc_v_out, rsum_out,
     tok, enc, dec, dbias, lat, gside, grad, gpre,
     keep, half, rs_wide, relay, rs_z, pre,
     rb, rb_low, rs_xy, norm_lane, norm_col,
-    m_old, v_old, w_new, m_new, v_new,
-    load_sem, store_sem, send_sem, recv_sem,
+    m_old, v_old, ebias_ref, dbias_ref, load_sem, send_sem, recv_sem,
 ):
     rows, width = acts_hbm.shape
     latents = enc_hbm.shape[1]
@@ -131,7 +131,9 @@
             (
                 (acts_hbm, tok.at[0, span(r * rows, rows)]),
                 (enc_hbm, enc.at[0]), (dec_hbm, dec.at[0]),
-                (m_hbm, m_old), (v_hbm, v_old),
+                (dec_m_hbm, m_old), (dec_v_hbm, v_old), (enc_hbm, enc_out),
+                (enc_m_hbm, enc_m_out), (enc_v_hbm, enc_v_out), (ebias_hbm, ebias_ref),
+                (dbias_hbm, dbias_ref),
             )
         )
     ]
@@ -141,15 +143,21 @@
     ]
     for to in greeted:
         pl.semaphore_signal(barrier, inc=1, device_id=to, device_id_type=MESH)
-    for load in loads:
+    for load in loads[:3]:
+        load.start()
+    for load in loads[8:]:
         load.start()
     loads[0].wait()
     loads[1].wait()
     keep[0] = dot_nn(tok[0, side_rows(r, c)], enc[0])
+    for load in loads[8:]:
+        load.wait()
     dbias[0] = jnp.concatenate(
         [dbias_ref[n : n + 1, :] for n in range(width // LANES)], axis=1
     )
     loads[2].wait()
+    for load in loads[3:8]:
+        load.start()
     pl.semaphore_wait(barrier, len(greeted))
 
     give, mine = side_rows(r, 1 - c), side_rows(r, c)
@@ -287,8 +295,7 @@
     strength = row_scale * strength
     penalty = jnp.concatenate([strength[n : n + 1, :] for n in range(lines)], axis=1)
     arrived([acts_back])
-    stores = [pltpu.make_async_copy(tok.at[0], tok_out, store_sem.at[0])]
-    stores[0].start()
+    tok_out[...] = tok[0]
 
     arrived(gather_own)
     for h in range(2):
@@ -307,8 +314,8 @@
     ]
     for h in range(2):
         grad[side_rows(h, c)] = gside[0, h * side : (h + 1) * side]
-    loads[3].wait()
-    loads[4].wait()
+    for load in loads[3:8]:
+        load.wait()
     arrived(lat_copies)
     arrived(grad_copies)
     ones_rows = jnp.ones((total_rows, LANES), BF16)
@@ -335,13 +342,6 @@
 
     gathers = [back(h, scatters[h]) for h in range(2)]
     lax.fori_loop(lines // 2, lines, decoder_block, 0)
-    stores += [
-        pltpu.make_async_copy(w_new, w_out, store_sem.at[1]),
-        pltpu.make_async_copy(m_new, m_out, store_sem.at[2]),
-        pltpu.make_async_copy(v_new, v_out, store_sem.at[3]),
-    ]
-    for store in stores[1:]:
-        store.start()
     row_sum = dot_nn(jnp.ones((8, total_rows), BF16), grad[...])
     rsum_out[...] = jnp.concatenate(
         [row_sum[0:1, n * LANES : (n + 1) * LANES] for n in range(width // LANES)], axis=0
@@ -351,17 +351,17 @@
         arrived(gathers[h])
         ref = gpre.at[side_rows(h, c)]
         last.append(send(ref, ref, pair))
-    arrived(last)
-    stores.append(pltpu.make_async_copy(gpre, gpre_out, store_sem.at[4]))
-    stores[-1].start()
+    for h in range(2):
+        gpre_out[side_rows(h, c)] = gpre[side_rows(h, c)]
     for copy in sent:
         copy.wait_send()
-    for store in stores:
-        store.wait()
+    for h in range(2):
+        arrived(last[h : h + 1])
+        gpre_out[side_rows(h, 1 - c)] = gpre[side_rows(h, 1 - c)]
     assert count[0] == SENDS
 
 
-def exchange(acts, enc_weight, dec_weight, dec_first, dec_second, enc_bias, dec_bias):
+def exchange(acts, enc_weight, dec_weight, dec_m, dec_v, enc_m, enc_v, enc_bias, dec_bias):
     rows, width = acts.shape
     latents = enc_weight.shape[1]
     total_rows = 2 * rows
@@ -376,13 +376,12 @@
         out_shape=(
             jax.ShapeDtypeStruct((total_rows, width), BF16),
             jax.ShapeDtypeStruct((total_rows, latents), BF16),
-            jax.ShapeDtypeStruct(dec_shape, BF16),
-            jax.ShapeDtypeStruct(dec_shape, BF16),
-            jax.ShapeDtypeStruct(dec_shape, BF16),
+            *[jax.ShapeDtypeStruct(dec_shape, BF16)] * 3,
+            *[jax.ShapeDtypeStruct(enc_weight.shape, BF16)] * 3,
             jax.ShapeDtypeStruct((width // LANES, LANES), F32),
         ),
-        in_specs=[hbm] * 5 + [vmem] * 2,
-        out_specs=(hbm,) * 5 + (vmem,),
+        in_specs=[hbm] * 9,
+        out_specs=(vmem,) * 9,
         scratch_shapes=[
             pltpu.VMEM((2, total_rows, width), BF16),
             pltpu.VMEM((2, width, latents), BF16),
@@ -403,41 +402,55 @@
             pltpu.VMEM((2, SIDE * SIDE, piece, width), BF16),
             pltpu.VMEM((CHIPS, 8, LANES), F32),
             pltpu.VMEM((latents, LANES), F32),
-            *[pltpu.VMEM(dec_shape, BF16)] * 5,
-            pltpu.SemaphoreType.DMA((5,)),
-            pltpu.SemaphoreType.DMA((5,)),
+            *[pltpu.VMEM(dec_shape, BF16)] * 2,
+            pltpu.VMEM(enc_bias.shape, F32),
+            pltpu.VMEM(dec_bias.shape, F32),
+            pltpu.SemaphoreType.DMA((10,)),
             pltpu.SemaphoreType.DMA((SENDS,)),
             pltpu.SemaphoreType.DMA((SENDS,)),
         ],
         compiler_params=pltpu.CompilerParams(
-            collective_id=0, has_side_effects=True, vmem_limit_bytes=60 << 20
+            collective_id=0, has_side_effects=True, vmem_limit_bytes=30 << 20
         ),
-    )(acts, enc_weight, dec_weight, dec_first, dec_second, enc_bias, dec_bias)
+    )(acts, enc_weight, dec_weight, dec_m, dec_v, enc_m, enc_v, enc_bias, dec_bias)
 
 
 def finish_kernel(
-    tok_ref, gpre_ref, w, m, v, rsum_ref, w_done, m_done, v_done,
-    w_next, m_next, v_next, bsum_out, rsum_out, w_out, m_out, v_out,
+    tok_ref, gpre_ref, w_done, m_done, v_done, w, m, v, rsum_ref,
+    w_next, m_next, v_next, bsum_out, rsum_out, w_out, m_out, v_out, sem,
 ):
-    @pl.when(pl.program_id(0) == 0)
+    blocks = pl.num_programs(0)
+    step = pl.program_id(0)
+    copies = [
+        pltpu.make_async_copy(src, dst, sem.at[n])
+        for n, (src, dst) in enumerate(((w_done, w_out), (m_done, m_out), (v_done, v_out)))
+    ]
+
+    @pl.when(step == 0)
     def _():
+        for copy in copies:
+            copy.start()
         total = dot_nn(jnp.ones((8, gpre_ref.shape[0]), BF16), gpre_ref[...])
         for n in range(bsum_out.shape[0]):
             bsum_out[n : n + 1, :] = total[0:1, n * LANES : (n + 1) * LANES]
         rsum_out[...] = rsum_ref[...]
 
-    gradient = dot_tn(tok_ref[...], gpre_ref[...])
-    w_next[...], m_next[...], v_next[...] = adam_step(w[...], m[...], v[...], gradient)
-    w_out[...] = w_done[...]
-    m_out[...] = m_done[...]
-    v_out[...] = v_done[...]
-
-
-def finish(tok, gpre, w, m, v, row_sum, decoder, blocks=4):
-    total_rows, latents = gpre.shape
-    width = w.shape[0]
+    size = w_next.shape[0]
+    at = pl.ds(pl.multiple_of(step * size, size), size)
+    gradient = dot_tn(tok_ref[:, at], gpre_ref[...])
+    w_next[...], m_next[...], v_next[...] = adam_step(w[at], m[at], v[at], gradient)
+
+    @pl.when(step == blocks - 1)
+    def _():
+        for copy in copies:
+            copy.wait()
+
+
+def finish(tok, gpre, decoder, encoder, row_sum, blocks=4):
+    latents, width = decoder[0].shape
     block = pl.BlockSpec((width // blocks, latents), lambda i: (i, 0))
-    turned = pl.BlockSpec((latents // blocks, width), lambda i: (i, 0))
+    vmem = pl.BlockSpec(memory_space=pltpu.VMEM)
+    hbm = pl.BlockSpec(memory_space=pltpu.HBM)
 
     def whole(shape):
         return pl.BlockSpec(shape, lambda i: (0, 0))
@@ -447,29 +460,32 @@
         finish_kernel,
         name="finish",
         grid=(blocks,),
-        out_shape=(jax.ShapeDtypeStruct(w.shape, BF16),) * 3
+        out_shape=(jax.ShapeDtypeStruct((width, latents), BF16),) * 3
         + tuple(jax.ShapeDtypeStruct(s, F32) for s in shapes)
-        + (jax.ShapeDtypeStruct(decoder[0].shape, BF16),) * 3,
-        in_specs=[
-            pl.BlockSpec((total_rows, width // blocks), lambda i: (0, i)),
-            whole((total_rows, latents)), block, block, block, whole(shapes[1]),
-            turned, turned, turned,
-        ],
-        out_specs=(block,) * 3 + tuple(whole(s) for s in shapes) + (turned,) * 3,
-        compiler_params=pltpu.CompilerParams(vmem_limit_bytes=56 << 20),
-    )(tok, gpre, w, m, v, row_sum, *decoder)
+        + (jax.ShapeDtypeStruct((latents, width), BF16),) * 3,
+        in_specs=[vmem] * 9,
+        out_specs=(block,) * 3 + tuple(whole(s) for s in shapes) + (hbm,) * 3,
+        scratch_shapes=[pltpu.SemaphoreType.DMA((3,))],
+        compiler_params=pltpu.CompilerParams(vmem_limit_bytes=40 << 20),
+    )(tok, gpre, *decoder, *encoder, row_sum)
 
 
 def local(
     model_acts, enc_weight, dec_weight, enc_bias, dec_bias,
     enc_first, enc_second, dec_first, dec_second,
 ):
-    tok, gpre, *decoder, row_sum = exchange(
-        model_acts, enc_weight, dec_weight, dec_first, dec_second,
-        enc_bias.reshape(-1, LANES), dec_bias.reshape(-1, LANES),
-    )
-    encoder = finish(tok, gpre, enc_weight, enc_first, enc_second, row_sum, decoder)
-    enc_next, enc_m, enc_v, bias_sum, row_sum, dec_next, dec_m, dec_v = encoder
+    moments = dec_first, dec_second, enc_first, enc_second
+    biases = enc_bias.reshape(-1, LANES), dec_bias.reshape(-1, LANES)
+    results = exchange(
+        *(
+            pltpu.with_memory_space_constraint(a, pltpu.HBM)
+            for a in (model_acts, enc_weight, dec_weight, *moments, *biases)
+        )
+    )
+    tok, gpre, row_sum = results[0], results[1], results[8]
+    enc_next, enc_m, enc_v, bias_sum, row_sum, dec_next, dec_m, dec_v = finish(
+        tok, gpre, results[2:5], results[5:8], row_sum
+    )
     return (
         enc_next, dec_next, enc_m, enc_v, dec_m, dec_v,
         bias_sum.reshape(-1), row_sum.reshape(-1),

time: 86 us -> 80.4 us (0.935)
  Pallas kernels: 85.2 us -> 79.6 us
    pallas_call x1, Pallas kernels: 6.84 us -> 3.56 us  [finish(): pl.pallas_call(finish_kernel, name='finish', grid=(blocks,), out_shape=(j...]
    pallas_call x1, Pallas kernels: 78.3 us -> 76.1 us  [exchange(): pl.pallas_call(exchange_kernel, name='exchange', out_shape=(jax.ShapeDtyp...]
where the time goes in v3:
time: 80.4 us; the launch traced here: 80.3 us
  Pallas kernels  79.6 us (99%)
    pallas_call x1, Pallas kernels, exchange(): pl.pallas_call(exchange_kernel, name='exchange', out_shape=(jax.ShapeDtyp...  76.1 us
    pallas_call x1, Pallas kernels, finish(): pl.pallas_call(finish_kernel, name='finish', grid=(blocks,), out_shape=(j...  3.56 us

profile of v3, /device:TPU:1, one launch (start us, length us, event | category | flops | bytes accessed | tf_op | source)
XLA Modules:
  0.0 80.3 jit_solution(7133035657198093642)
XLA Ops:
  0.6 76.1 %exchange.1 = (bf16[512,512]{1,0:T(8,128)(2,1)S(1)}, bf16[512,768]{1,0:T(8,128)(2,1)S(1)}, bf16[768,512]{1,0:T(8,128)(2,1)S(1)}, bf16[768,512]{1,0:T(8,128)(2,1)...) custom-call(bf16[256,512]{1,0:T(8,128)(2,1)} %acts_hbm.1, ...), custom_call_target="tpu_custom_call" | custom-call | tf_op jit(solution)/shard_map/exchange/pallas_call | solution.py:373
  76.7 3.6 %finish.1 = (bf16[512,768]{1,0:T(8,128)(2,1)}, bf16[512,768]{1,0:T(8,128)(2,1)}, bf16[512,768]{1,0:T(8,128)(2,1)}, f32[6,128]{1,0:T(8,128)}, f32[4,128]{1,0:T(4,...) custom-call(bf16[512,512]{1,0:T(8,128)(2,1)S(1)} %get-tuple-element.25.tok_ref, ...), custom_call_target="tpu_custom_call" | custom-call | tf_op jit(solution)/shard_map/finish/pallas_call | solution.py:459

commit v4 on v3

--- a/solution.py
+++ b/solution.py
@@ -24,6 +24,7 @@
 SIDE = 4
 LANES = 128
 SENDS = 136
+EARLY, LATE = 2, 5
 FAR_Z = (4, 3, 5, 2, 6, 1, 7)
 FAR_XY = tuple(
     sorted(
@@ -73,6 +74,7 @@
     side = rows // 2
     piece = side // CHIPS
     lines = latents // LANES
+    part = 2 * side // (SIDE * SIDE)
     row_scale = sparsity / total_rows
 
     e, l, r = (lax.axis_index(a) for a in ("expert", "latent", "row"))
@@ -143,32 +145,40 @@
     ]
     for to in greeted:
         pl.semaphore_signal(barrier, inc=1, device_id=to, device_id_type=MESH)
-    for load in loads[:3]:
+    for load in loads[:3] + loads[8:]:
         load.start()
-    for load in loads[8:]:
+    pl.semaphore_wait(barrier, len(greeted))
+
+    give = side_rows(r, 1 - c)
+    give_hbm = acts_hbm.at[span((1 - c) * side, side)]
+    acts_far = [
+        send(acts_hbm.at[span(c * side, side)], tok.at[0, side_rows(r, c)], mirror),
+        send(give_hbm, tok.at[1, give], mirror_pair),
+    ]
+    acts_pair = send(give_hbm, tok.at[1, give], pair)
+    enc_pair = send(enc_hbm, enc.at[1], pair)
+    for load in loads[3:8]:
         load.start()
-    loads[0].wait()
-    loads[1].wait()
-    keep[0] = dot_nn(tok[0, side_rows(r, c)], enc[0])
     for load in loads[8:]:
         load.wait()
     dbias[0] = jnp.concatenate(
         [dbias_ref[n : n + 1, :] for n in range(width // LANES)], axis=1
     )
-    loads[2].wait()
-    for load in loads[3:8]:
-        load.start()
-    pl.semaphore_wait(barrier, len(greeted))
-
-    give, mine = side_rows(r, 1 - c), side_rows(r, c)
-    acts_pair = send(tok.at[0, give], tok.at[1, give], pair)
-    enc_pair = send(enc.at[0], enc.at[1], pair)
-    acts_far = [
-        send(tok.at[0, mine], tok.at[0, mine], mirror),
-        send(tok.at[0, give], tok.at[1, give], mirror_pair),
-    ]
-    dec_pair = send(dec.at[0], dec.at[1], pair)
-    bias_pair = send(dbias.at[0], dbias.at[1], pair)
+    for load in loads[:2]:
+        load.wait()
+
+    ones_lane = jnp.ones((8, width), BF16)
+    ones_col = jnp.ones((width, LANES), BF16)
+
+    def squares(f):
+        wide = dec[f].astype(F32)
+        square = wide * wide
+        high = square.astype(BF16)
+        low = (square - high.astype(F32)).astype(BF16)
+        return (
+            dot_nt(ones_lane, high) + dot_nt(ones_lane, low),
+            dot_nn(high, ones_col) + dot_nn(low, ones_col),
+        )
 
     def z_part(values, step):
         return values.at[span(at_z(step) * piece, piece)]
@@ -196,29 +206,25 @@
         at = own_piece(h)
         return [send(buf.at[at], buf.at[at], z_peer(s)) for s in FAR_Z]
 
-    arrived([acts_pair, enc_pair])
-    keep[0] = keep[0] + dot_nn(tok[1, mine], enc[1])
-    first = relay_start(keep.at[0], rs_wide.at[0], 1)
-    arrived(acts_far)
+    arrived([acts_pair, enc_pair, *acts_far])
+    encoded = []
+    for h, s in enumerate((1, -1)):
+        at = side_rows(h, c)
+        keep[h] = dot_nn(tok[0, at], enc[0]) + dot_nn(tok[1, at], enc[1])
+        encoded.append(relay_start(keep.at[h], rs_wide.at[h], s))
+    bias_pair = send(dbias.at[0], dbias.at[1], pair)
+    dec_pair = send(dec_hbm, dec.at[1], pair)
+    loads[2].wait()
     theirs = side_rows(1 - r, c)
-    keep[1] = dot_nn(tok[0, theirs], enc[0]) + dot_nn(tok[1, theirs], enc[1])
-    second = relay_start(keep.at[1], rs_wide.at[1], -1)
-    first = relay_pass(keep.at[0], rs_wide.at[0], relay.at[0], first, 1)
-    second = relay_pass(keep.at[1], rs_wide.at[1], relay.at[1], second, -1)
     acts_back = send(tok.at[1, theirs], tok.at[0, theirs], pair)
-
-    ones_lane = jnp.ones((8, width), BF16)
-    ones_col = jnp.ones((width, LANES), BF16)
+    for h, s in enumerate((1, -1)):
+        encoded[h] = relay_pass(keep.at[h], rs_wide.at[h], relay.at[h], encoded[h], s)
+
+    lane, column = squares(0)
     arrived([dec_pair, bias_pair])
-    lane, column = norm_eps, norm_eps
-    for f in range(2):
-        wide = dec[f].astype(F32)
-        square = wide * wide
-        high = square.astype(BF16)
-        low = (square - high.astype(F32)).astype(BF16)
-        lane = lane + (dot_nt(ones_lane, high) + dot_nt(ones_lane, low))
-        column = column + (dot_nn(high, ones_col) + dot_nn(low, ones_col))
-    norm_col[...] = jnp.sqrt(column)
+    more_lane, more_column = squares(1)
+    lane = lane + more_lane + norm_eps
+    norm_col[...] = jnp.sqrt(column + more_column + norm_eps)
     norm_lane[0] = jnp.sqrt(
         jnp.concatenate(
             [lane[0:1, n * LANES : (n + 1) * LANES] for n in range(lines)]
@@ -231,89 +237,79 @@
         [ebias_ref[pl.ds(r * lines + n, 1), :] for n in range(lines)], axis=1
     )
 
-    def encode(k, h, copies):
-        arrived(copies)
-        value = keep[k, span(z * piece, piece)] + bias
+    def encode(h):
+        arrived(encoded[h])
+        value = keep[h, span(z * piece, piece)] + bias
         for n in range(3, 7):
-            value = value + rs_wide[k, n]
+            value = value + rs_wide[h, n]
         pre[h] = value
         lat[own_piece(h)] = jnp.maximum(value, 0.0).astype(BF16)
         return z_gather(lat, h)
 
-    first = encode(0, r, first)
-    second = encode(1, 1 - r, second)
-
-    def rebuild(f, h):
-        at = span(h * side, side)
-        part = dot_nn(lat[side_rows(h, c)], dec[f])
-        rb[f, at] = part
-        rb_low[f, at] = part.astype(BF16)
-
-    def plane_scatter(f):
+    gathers = [encode(h) for h in range(2)]
+
+    def block(buf, h, place):
+        return buf.at[h, lax.rem(place, 2), span(lax.div(place, 2) * part, part)]
+
+    place = x * SIDE + y
+    feature = lax.rem(place, 2)
+
+    def rebuild(h):
+        arrived(gathers[h])
+        acts = lat[side_rows(h, c)]
+        for f in range(2):
+            product = dot_nn(acts, dec[f])
+            rb[h, f] = product
+            rb_low[h, f] = product.astype(BF16)
         copies = []
         for dx, dy in FAR_XY:
             px, py = at_xy(dx, dy)
-            at = span((px * SIDE + py) * piece, piece)
+            piece_low = block(rb_low, h, px * SIDE + py)
             copies.append(
-                send(rb_low.at[f, at], rs_xy.at[f, dx * SIDE + dy], xy_peer(dx, dy))
+                send(piece_low, rs_xy.at[h, dx * SIDE + dy], xy_peer(dx, dy))
             )
         return copies
 
-    arrived(first)
-    rebuild(0, r)
-    arrived(second)
-    rebuild(0, 1 - r)
-    scatter_own = plane_scatter(0)
-    rebuild(1, r)
-    rebuild(1, 1 - r)
-    scatter_pair = plane_scatter(1)
+    scatters = [rebuild(h) for h in range(2)]
     lat_copies = [
         send(lat.at[side_rows(h, c)], lat.at[side_rows(h, c)], pair) for h in range(2)
     ]
 
-    place = x * SIDE + y
-    at_place = span(place * piece, piece)
-    from_rows = lax.div(place, CHIPS) * rows + c * side + lax.rem(place, CHIPS) * piece
-
-    def residual(f, copies):
-        arrived(copies)
-        total = rb[f, at_place]
+    def residual(h):
+        arrived(scatters[h])
+        total = block(rb, h, place)[...]
         for n in range(1, SIDE * SIDE):
-            total = total + rs_xy[f, n].astype(F32)
-        acts = tok[f, span(from_rows, piece)].astype(F32)
-        grad_rows = 2.0 * (total + dbias[f] - acts) / total_rows
-        gside[f, at_place] = grad_rows.astype(BF16)
-        ref = gside.at[f, at_place]
+            total = total + rs_xy[h, n].astype(F32)
+        from_rows = span(h * rows + c * side + lax.div(place, 2) * part, part)
+        acts = tok[feature, from_rows].astype(F32)
+        grad_rows = 2.0 * (total + dbias[feature] - acts) / total_rows
+        ref = block(gside, h, place)
+        ref[...] = grad_rows.astype(BF16)
         return [send(ref, ref, xy_peer(*s)) for s in FAR_XY]
 
-    gather_own = residual(0, scatter_own)
-    gather_pair = residual(1, scatter_pair)
+    gathers = [residual(h) for h in range(2)]
     arrived(norm_copies)
     strength = norm_lane[0]
     for s in range(1, CHIPS):
         strength = strength + norm_lane[s]
     strength = row_scale * strength
     penalty = jnp.concatenate([strength[n : n + 1, :] for n in range(lines)], axis=1)
+    def back_start(h):
+        arrived(gathers[h])
+        total = dot_nt(gside[h, 0], dec[0]) + dot_nt(gside[h, 1], dec[1])
+        keep[2 + h] = total
+        half[h] = total.astype(BF16)
+        return z_scatter(half.at[h], rs_z.at[h])
+
+    scatters = [back_start(h) for h in range(2)]
+
+    grad_copies = [
+        send(gside.at[h, 1], grad.at[side_rows(h, c)], pair) for h in range(2)
+    ]
+    for h in range(2):
+        grad[side_rows(h, c)] = gside[h, 0]
     arrived([acts_back])
     tok_out[...] = tok[0]
-
-    arrived(gather_own)
-    for h in range(2):
-        keep[2 + h] = dot_nt(gside[0, h * side : (h + 1) * side], dec[0])
-    arrived(gather_pair)
-    scatters = []
-    for h in range(2):
-        total = keep[2 + h] + dot_nt(gside[1, h * side : (h + 1) * side], dec[1])
-        keep[2 + h] = total
-        half[h] = total.astype(BF16)
-        scatters.append(z_scatter(half.at[h], rs_z.at[h]))
-
-    grad_copies = [
-        send(gside.at[1, span(h * side, side)], grad.at[side_rows(h, c)], pair)
-        for h in range(2)
-    ]
-    for h in range(2):
-        grad[side_rows(h, c)] = gside[0, h * side : (h + 1) * side]
     for load in loads[3:8]:
         load.wait()
     arrived(lat_copies)
@@ -330,27 +326,29 @@
         w_new[at], m_new[at], v_new[at] = adam_step(weight, m_old[at], v_old[at], gradient)
         return carry
 
-    lax.fori_loop(0, lines // 2, decoder_block, 0)
-
-    def back(h, copies):
-        arrived(copies)
+    def back(h):
+        arrived(scatters[h])
         value = keep[2 + h, span(z * piece, piece)] + penalty
         for s in range(1, CHIPS):
             value = value + rs_z[h, s].astype(F32)
         gpre[own_piece(h)] = jnp.where(pre[h] > 0, value, 0.0).astype(BF16)
         return z_gather(gpre, h)
 
-    gathers = [back(h, scatters[h]) for h in range(2)]
-    lax.fori_loop(lines // 2, lines, decoder_block, 0)
+    def forward(h):
+        arrived(gathers[h])
+        ref = gpre.at[side_rows(h, c)]
+        return send(ref, ref, pair)
+
+    lax.fori_loop(0, EARLY, decoder_block, 0)
+    gathers = [back(h) for h in range(2)]
+    lax.fori_loop(EARLY, LATE, decoder_block, 0)
+    last = [forward(0)]
+    lax.fori_loop(LATE, lines, decoder_block, 0)
+    last.append(forward(1))
     row_sum = dot_nn(jnp.ones((8, total_rows), BF16), grad[...])
     rsum_out[...] = jnp.concatenate(
         [row_sum[0:1, n * LANES : (n + 1) * LANES] for n in range(width // LANES)], axis=0
     )
-    last = []
-    for h in range(2):
-        arrived(gathers[h])
-        ref = gpre.at[side_rows(h, c)]
-        last.append(send(ref, ref, pair))
     for h in range(2):
         gpre_out[side_rows(h, c)] = gpre[side_rows(h, c)]
     for copy in sent:
@@ -367,6 +365,7 @@
     total_rows = 2 * rows
     side = rows // 2
     piece = side // CHIPS
+    part = 2 * side // (SIDE * SIDE)
     hbm = pl.BlockSpec(memory_space=pltpu.HBM)
     vmem = pl.BlockSpec(memory_space=pltpu.VMEM)
     dec_shape = (latents, width)
@@ -388,7 +387,7 @@
             pltpu.VMEM((2, *dec_shape), BF16),
             pltpu.VMEM((2, 1, width), F32),
             pltpu.VMEM((total_rows, latents), BF16),
-            pltpu.VMEM((2, rows, width), BF16),
+            pltpu.VMEM((2, 2, side, width), BF16),
             pltpu.VMEM((total_rows, width), BF16),
             pltpu.VMEM((total_rows, latents), BF16),
             pltpu.VMEM((4, side, latents), F32),
@@ -397,9 +396,9 @@
             pltpu.VMEM((2, 2, piece, latents), F32),
             pltpu.VMEM((2, CHIPS, piece, latents), BF16),
             pltpu.VMEM((2, piece, latents), F32),
-            pltpu.VMEM((2, rows, width), F32),
-            pltpu.VMEM((2, rows, width), BF16),
-            pltpu.VMEM((2, SIDE * SIDE, piece, width), BF16),
+            pltpu.VMEM((2, 2, side, width), F32),
+            pltpu.VMEM((2, 2, side, width), BF16),
+            pltpu.VMEM((2, SIDE * SIDE, part, width), BF16),
             pltpu.VMEM((CHIPS, 8, LANES), F32),
             pltpu.VMEM((latents, LANES), F32),
             *[pltpu.VMEM(dec_shape, BF16)] * 2,
@@ -446,7 +445,7 @@
             copy.wait()
 
 
-def finish(tok, gpre, decoder, encoder, row_sum, blocks=4):
+def finish(tok, gpre, decoder, encoder, row_sum, blocks=2):
     latents, width = decoder[0].shape
     block = pl.BlockSpec((width // blocks, latents), lambda i: (i, 0))
     vmem = pl.BlockSpec(memory_space=pltpu.VMEM)

time: 80.4 us -> 77.5 us (0.964)
  Pallas kernels: 79.6 us -> 76.8 us
    pallas_call x1, Pallas kernels: 76.1 us -> 73.8 us  [exchange(): pl.pallas_call(exchange_kernel, name='exchange', out_shape=(jax.ShapeDtyp...]
where the time goes in v4:
time: 77.5 us; the launch traced here: 77.4 us
  Pallas kernels  76.8 us (99%)
    pallas_call x1, Pallas kernels, exchange(): pl.pallas_call(exchange_kernel, name='exchange', out_shape=(jax.ShapeDtyp...  73.8 us
    pallas_call x1, Pallas kernels, finish(): pl.pallas_call(finish_kernel, name='finish', grid=(blocks,), out_shape=(j...  2.96 us

profile of v4, /device:TPU:1, one launch (start us, length us, event | category | flops | bytes accessed | tf_op | source)
XLA Modules:
  0.0 77.4 jit_solution(6357697317314181101)
XLA Ops:
  0.6 73.8 %exchange.1 = (bf16[512,512]{1,0:T(8,128)(2,1)S(1)}, bf16[512,768]{1,0:T(8,128)(2,1)S(1)}, bf16[768,512]{1,0:T(8,128)(2,1)S(1)}, bf16[768,512]{1,0:T(8,128)(2,1)...) custom-call(bf16[256,512]{1,0:T(8,128)(2,1)} %acts_hbm.1, ...), custom_call_target="tpu_custom_call" | custom-call | tf_op jit(solution)/shard_map/exchange/pallas_call | solution.py:372
  74.4 3.0 %finish.1 = (bf16[512,768]{1,0:T(8,128)(2,1)}, bf16[512,768]{1,0:T(8,128)(2,1)}, bf16[512,768]{1,0:T(8,128)(2,1)}, f32[6,128]{1,0:T(8,128)}, f32[4,128]{1,0:T(4,...) custom-call(bf16[512,512]{1,0:T(8,128)(2,1)S(1)} %get-tuple-element.25.tok_ref, ...), custom_call_target="tpu_custom_call" | custom-call | tf_op jit(solution)/shard_map/finish/pallas_call | solution.py:458

commit v5 on v4

--- a/solution.py
+++ b/solution.py
@@ -23,6 +23,7 @@
 CHIPS = 8
 SIDE = 4
 LANES = 128
+ORIENT = (1, -1)
 SENDS = 136
 EARLY, LATE = 2, 5
 FAR_Z = (4, 3, 5, 2, 6, 1, 7)
@@ -157,6 +158,7 @@
     ]
     acts_pair = send(give_hbm, tok.at[1, give], pair)
     enc_pair = send(enc_hbm, enc.at[1], pair)
+    dec_pair = send(dec_hbm, dec.at[1], pair)
     for load in loads[3:8]:
         load.start()
     for load in loads[8:]:
@@ -206,6 +208,31 @@
         at = own_piece(h)
         return [send(buf.at[at], buf.at[at], z_peer(s)) for s in FAR_Z]
 
+    def near_gather(buf, h, s):
+        at = own_piece(h)
+        return [send(buf.at[at], buf.at[at], z_peer(n)) for n in (2 * s, -2 * s, -s, s)]
+
+    def far_gather(buf, h, copies, s):
+        def piece_of(step):
+            return buf.at[span(h * rows + c * side + at_z(step) * piece, piece)]
+
+        arrived(copies[1:2])
+        far = [send(piece_of(2 * s), piece_of(2 * s), z_peer(n * s)) for n in (-2, -1)]
+        arrived(copies[:1])
+        far.append(send(piece_of(-2 * s), piece_of(-2 * s), z_peer(s)))
+        return copies[2:] + far
+
+    loads[2].wait()
+    lane, column = squares(0)
+    arrived([dec_pair])
+    more_lane, more_column = squares(1)
+    norm_col[...] = jnp.sqrt(column + more_column + norm_eps)
+    lane = jnp.sqrt(lane + more_lane + norm_eps)
+    norm_lane[0] = jnp.concatenate(
+        [lane[0:1, n * LANES : (n + 1) * LANES] for n in range(lines)]
+        + [jnp.zeros((8 - lines, LANES), F32)],
+        axis=0,
+    )
     arrived([acts_pair, enc_pair, *acts_far])
     encoded = []
     for h, s in enumerate((1, -1)):
@@ -213,26 +240,13 @@
         keep[h] = dot_nn(tok[0, at], enc[0]) + dot_nn(tok[1, at], enc[1])
         encoded.append(relay_start(keep.at[h], rs_wide.at[h], s))
     bias_pair = send(dbias.at[0], dbias.at[1], pair)
-    dec_pair = send(dec_hbm, dec.at[1], pair)
-    loads[2].wait()
     theirs = side_rows(1 - r, c)
     acts_back = send(tok.at[1, theirs], tok.at[0, theirs], pair)
     for h, s in enumerate((1, -1)):
         encoded[h] = relay_pass(keep.at[h], rs_wide.at[h], relay.at[h], encoded[h], s)
 
-    lane, column = squares(0)
-    arrived([dec_pair, bias_pair])
-    more_lane, more_column = squares(1)
-    lane = lane + more_lane + norm_eps
-    norm_col[...] = jnp.sqrt(column + more_column + norm_eps)
-    norm_lane[0] = jnp.sqrt(
-        jnp.concatenate(
-            [lane[0:1, n * LANES : (n + 1) * LANES] for n in range(lines)]
-            + [jnp.zeros((8 - lines, LANES), F32)],
-            axis=0,
-        )
-    )
     norm_copies = [send(norm_lane.at[0], norm_lane.at[s], z_peer(s)) for s in FAR_Z]
+    arrived([bias_pair])
     bias = jnp.concatenate(
         [ebias_ref[pl.ds(r * lines + n, 1), :] for n in range(lines)], axis=1
     )
@@ -332,7 +346,7 @@
         for s in range(1, CHIPS):
             value = value + rs_z[h, s].astype(F32)
         gpre[own_piece(h)] = jnp.where(pre[h] > 0, value, 0.0).astype(BF16)
-        return z_gather(gpre, h)
+        return near_gather(gpre, h, ORIENT[h])
 
     def forward(h):
         arrived(gathers[h])
@@ -341,6 +355,7 @@
 
     lax.fori_loop(0, EARLY, decoder_block, 0)
     gathers = [back(h) for h in range(2)]
+    gathers = [far_gather(gpre, h, gathers[h], ORIENT[h]) for h in range(2)]
     lax.fori_loop(EARLY, LATE, decoder_block, 0)
     last = [forward(0)]
     lax.fori_loop(LATE, lines, decoder_block, 0)

time: 77.5 us -> 76.9 us (level)
  no operation moved by 1% of the time
where the time goes in v5:
time: 76.9 us
  Pallas kernels  76.2 us (99%)
    pallas_call x1, Pallas kernels, exchange(): pl.pallas_call(exchange_kernel, name='exchange', out_shape=(jax.ShapeDtyp...  73.3 us
    pallas_call x1, Pallas kernels, finish(): pl.pallas_call(finish_kernel, name='finish', grid=(blocks,), out_shape=(j...  2.96 us

profile of v5, /device:TPU:1, one launch (start us, length us, event | category | flops | bytes accessed | tf_op | source)
XLA Modules:
  0.0 76.9 jit_solution(17576595635122735620)
XLA Ops:
  0.6 73.3 %exchange.1 = (bf16[512,512]{1,0:T(8,128)(2,1)S(1)}, bf16[512,768]{1,0:T(8,128)(2,1)S(1)}, bf16[768,512]{1,0:T(8,128)(2,1)S(1)}, bf16[768,512]{1,0:T(8,128)(2,1)...) custom-call(bf16[256,512]{1,0:T(8,128)(2,1)} %acts_hbm.1, ...), custom_call_target="tpu_custom_call" | custom-call | tf_op jit(solution)/shard_map/exchange/pallas_call | solution.py:387
  73.9 3.0 %finish.1 = (bf16[512,768]{1,0:T(8,128)(2,1)}, bf16[512,768]{1,0:T(8,128)(2,1)}, bf16[512,768]{1,0:T(8,128)(2,1)}, f32[6,128]{1,0:T(8,128)}, f32[4,128]{1,0:T(4,...) custom-call(bf16[512,512]{1,0:T(8,128)(2,1)S(1)} %get-tuple-element.25.tok_ref, ...), custom_call_target="tpu_custom_call" | custom-call | tf_op jit(solution)/shard_map/finish/pallas_call | solution.py:473
